TPU v7x, 32 devices: a whole 2x2x4 slice. The times are simulated.
32 devices in a mesh: dp: 4 (over z), row: 4 (over x, core), col: 2 (over y).
Axes of the slice: x: 2, y: 2, z: 4, core: 2. Of those that a mesh axis runs over, the one named last changes fastest.
Arguments:
- tokens: bfloat16 [8, 4096, 1024], P('dp', ('row', 'col')), may hold values from -6 to 6
- cotangent: bfloat16 [8, 4096, 1024], P('dp', ('row', 'col')), may hold values from -6 to 6
- branch: int32 [8, 8], P('dp'), may hold values from 256 to 2048
- ln1_gain: float32 [1024], replicated, may hold values from 0.5 to 1.5
- ln1_bias: float32 [1024], replicated, may hold values from -1.2 to 1.2
- qkv_weight: bfloat16 [1024, 3, 1024], P('row', None, 'col'), may hold values from -0.1875 to 0.1875
- qv_bias: float32 [2, 1024], P(None, 'col'), may hold values from -1.2 to 1.2
- out_weight: bfloat16 [1024, 1024], P('col', 'row'), may hold values from -1.5 to 1.5
- out_bias: float32 [1024], replicated, may hold values from -1.2 to 1.2
- ln2_gain: float32 [1024], replicated, may hold values from 0.5 to 1.5
- ln2_bias: float32 [1024], replicated, may hold values from -1.2 to 1.2
- fc_weight: bfloat16 [1024, 4096], P('row', 'col'), may hold values from -0.1875 to 0.1875
- fc_bias: float32 [4096], P('col'), may hold values from -1.8 to 1.8
- proj_weight: bfloat16 [4096, 1024], P('col', 'row'), may hold values from -0.09375 to 0.09375
- proj_bias: float32 [1024], replicated, may hold values from -1.2 to 1.2
Outputs:
- block_out: bfloat16 [8, 4096, 1024], P('dp', ('row', 'col'))
- input_grad: float32 [8, 4096, 1024], P('dp', ('row', 'col'))
- d_ln1_gain: float32 [1024], replicated
- d_ln1_bias: float32 [1024], replicated
- d_qkv_weight: float32 [1024, 3, 1024], P(('dp', 'row'), None, 'col')
- d_qv_bias: float32 [2, 1024], replicated
- d_out_weight: float32 [1024, 1024], P('col', ('dp', 'row'))
- d_out_bias: float32 [1024], replicated
- d_ln2_gain: float32 [1024], replicated
- d_ln2_bias: float32 [1024], replicated
- d_fc_weight: float32 [1024, 4096], P(('dp', 'row'), 'col')
- d_fc_bias: float32 [4096], replicated
- d_proj_weight: float32 [4096, 1024], P('col', ('dp', 'row'))
- d_proj_bias: float32 [1024], replicated
Inputs may be any that keep to these rules, and one draw needn't show every extreme that they name: branch[g, c] is the number of leading prompt tokens that continuation c of group g sees.
All inputs are finite; a program needn't handle non-finite values.
Results may differ from a plain program's by a relative error of at most 0.015.
Values may be sent and summed in bfloat16 or wider, within the bound.
No kernel may reach another device: no remote copies, remote signals or barrier semaphores. Data moves between devices by JAX's collectives and lax.ppermute only.
A program may use at most 328 MiB of HBM per device.

v0:
```python
import jax
import jax.numpy as jnp
from jax import lax
from jax.sharding import PartitionSpec as P

HEAD = 64
PLEN = 2048
CLEN = 256
CONTS = 8
EPSILON = 1e-05
MASKED_SCORE = -1e30


def normalize(values, gain, shift):
    center = values - jnp.mean(values, axis=-1, keepdims=True)
    spread = jnp.mean(center * center, axis=-1, keepdims=True)
    return center * lax.rsqrt(spread + EPSILON) * gain + shift


def gelu_tanh(values):
    return jax.nn.gelu(values, approximate=True)


def allowed_keys(row_pos, col_pos, branch_cut):
    row_seg = jnp.where(row_pos >= PLEN, (row_pos - PLEN) // CLEN, -1)
    col_seg = jnp.where(col_pos >= PLEN, (col_pos - PLEN) // CLEN, -1)
    picked = (row_seg[:, None] == jnp.arange(CONTS, dtype=jnp.int32)[None, :]).astype(jnp.int32)
    row_cut = jnp.sum(picked * branch_cut[None, :], axis=1)
    causal = col_pos[None, :] <= row_pos[:, None]
    same_seq = col_seg[None, :] == row_seg[:, None]
    in_prefix = (
        (row_seg[:, None] >= 0) & (col_seg[None, :] < 0) & (col_pos[None, :] < row_cut[:, None])
    )
    return same_seq & causal | in_prefix


def add_trees(first, second):
    return jax.tree.map(lambda total, extra: total + extra, first, second)


def body(
    tokens,
    cotangent,
    branch,
    ln1_gain,
    ln1_bias,
    qkv_weight,
    qv_bias,
    out_weight,
    out_bias,
    ln2_gain,
    ln2_bias,
    fc_weight,
    fc_bias,
    proj_weight,
    proj_bias,
):
    scale = HEAD ** (-0.5)
    width = tokens.shape[2]
    local_rows = tokens.shape[1]
    head_cols = qv_bias.shape[1]
    head_count = head_cols // HEAD
    ff_local = fc_bias.shape[0]
    col_count = lax.axis_size("col")
    row_count = lax.axis_size("row")
    row_rows = local_rows * col_count
    group_rows = row_rows * row_count
    q_block = min(512, row_rows)
    block_count = row_rows // q_block
    row_base = lax.axis_index("row") * row_rows
    col_index = lax.axis_index("col")
    bias_three = jnp.stack([qv_bias[0], jnp.zeros_like(qv_bias[0]), qv_bias[1]])
    key_pos = jnp.arange(group_rows, dtype=jnp.int32)
    block_starts = jnp.arange(block_count, dtype=jnp.int32) * q_block

    def spread_rows(values):
        return lax.all_gather(values, "col", axis=0, tiled=True)

    def spread_grads(values):
        return lax.all_gather(values, "col", axis=0, tiled=True)

    def sum_branch(values):
        return lax.psum_scatter(values, "col", scatter_dimension=0, tiled=True)

    def sum_inputs(values):
        return lax.psum_scatter(values, "col", scatter_dimension=0, tiled=True)

    kept_weights = (
        lax.all_gather(qkv_weight, "row", axis=0, tiled=True),
        lax.all_gather(out_weight, "row", axis=1, tiled=True),
        lax.all_gather(fc_weight, "row", axis=0, tiled=True),
        lax.all_gather(proj_weight, "row", axis=1, tiled=True),
    )

    def block_scores(queries3, keys3, offset, branch_cut):
        q_part = lax.dynamic_slice_in_dim(queries3, offset, q_block, 0)
        row_pos = row_base + offset + jnp.arange(q_block, dtype=jnp.int32)
        allowed = allowed_keys(row_pos, key_pos, branch_cut)
        scores = (
            jnp.einsum("qhd,khd->hqk", q_part, keys3, preferred_element_type=jnp.float32) * scale
        )
        return (q_part, jnp.where(allowed[None], scores, MASKED_SCORE))

    def micro_step(carry, micro_item):
        grads_acc, small_acc = carry
        tok_rows, cot_rows, branch_cut = micro_item
        w_qkv, w_out, w_fc, w_proj = kept_weights
        residual = tok_rows.astype(jnp.float32)
        normed = normalize(residual, ln1_gain, ln1_bias).astype(jnp.bfloat16)
        normed_all = spread_rows(normed)
        projected = jnp.einsum("td,dsf->tsf", normed_all, w_qkv, preferred_element_type=jnp.float32)
        projected = (projected + bias_three[None]).astype(jnp.bfloat16)
        key_rows, value_rows = (
            lax.all_gather(projected[:, 1], "row", axis=0, tiled=True),
            lax.all_gather(projected[:, 2], "row", axis=0, tiled=True),
        )
        queries3 = projected[:, 0].reshape(row_rows, head_count, HEAD)
        keys3 = key_rows.reshape(group_rows, head_count, HEAD)
        values3 = value_rows.reshape(group_rows, head_count, HEAD)

        def attend(offset):
            q_part, scores = block_scores(queries3, keys3, offset, branch_cut)
            row_peak = jnp.max(scores, axis=-1, keepdims=True)
            exponent = jnp.exp(scores - row_peak)
            row_total = jnp.sum(exponent, axis=-1, keepdims=True)
            probs_low = (exponent / row_total).astype(jnp.bfloat16)
            mixed_rows = jnp.einsum(
                "hqk,khd->qhd", probs_low, values3, preferred_element_type=jnp.float32
            )
            return (mixed_rows, (row_peak + jnp.log(row_total))[..., 0])

        attended, log_totals = lax.map(attend, block_starts)
        attended = attended.reshape(row_rows, head_cols).astype(jnp.bfloat16)
        branch_part = jnp.dot(attended, w_out, preferred_element_type=jnp.float32)
        middle = residual + sum_branch(branch_part) + out_bias
        normed_two = normalize(middle, ln2_gain, ln2_bias).astype(jnp.bfloat16)
        normed_two_all = spread_rows(normed_two)
        hidden = jnp.dot(normed_two_all, w_fc, preferred_element_type=jnp.float32) + fc_bias
        active = gelu_tanh(hidden).astype(jnp.bfloat16)
        ffn_part = jnp.dot(active, w_proj, preferred_element_type=jnp.float32)
        output_rows = (middle + sum_branch(ffn_part) + proj_bias).astype(jnp.bfloat16)
        cot_all = spread_grads(cot_rows)
        grad_proj = jnp.einsum("tf,td->fd", active, cot_all, preferred_element_type=jnp.float32)
        grad_proj_bias = jnp.sum(cot_rows.astype(jnp.float32), axis=0)
        grad_active = jnp.einsum("td,fd->tf", cot_all, w_proj, preferred_element_type=jnp.float32)
        grad_hidden = jax.vjp(gelu_tanh, hidden)[1](grad_active)[0].astype(jnp.bfloat16)
        grad_fc = jnp.einsum(
            "td,tf->df", normed_two_all, grad_hidden, preferred_element_type=jnp.float32
        )
        grad_fc_bias = jnp.sum(grad_hidden.astype(jnp.float32), axis=0)
        grad_normed_two = sum_inputs(
            jnp.einsum("tf,df->td", grad_hidden, w_fc, preferred_element_type=jnp.float32)
        )
        back_middle, grad_gain_two, grad_bias_two = jax.vjp(normalize, middle, ln2_gain, ln2_bias)[
            1
        ](grad_normed_two)
        grad_middle = cot_rows.astype(jnp.float32) + back_middle
        grad_out_rows = grad_middle.astype(jnp.bfloat16)
        grad_out_all = spread_grads(grad_out_rows)
        grad_out = jnp.einsum(
            "tc,td->cd", attended, grad_out_all, preferred_element_type=jnp.float32
        )
        grad_out_bias = jnp.sum(grad_out_rows.astype(jnp.float32), axis=0)
        grad_att = jnp.einsum("td,cd->tc", grad_out_all, w_out, preferred_element_type=jnp.float32)
        grad_att = grad_att.astype(jnp.bfloat16).reshape(row_rows, head_count, HEAD)

        def attend_back(acc_pair, block_item):
            offset, log_total = block_item
            grad_keys_acc, grad_values_acc = acc_pair
            q_part, scores = block_scores(queries3, keys3, offset, branch_cut)
            probs = jnp.exp(scores - log_total[..., None])
            probs_low = probs.astype(jnp.bfloat16)
            grad_part = lax.dynamic_slice_in_dim(grad_att, offset, q_block, 0)
            grad_values_acc = grad_values_acc + jnp.einsum(
                "hqk,qhd->khd", probs_low, grad_part, preferred_element_type=jnp.float32
            )
            grad_probs = jnp.einsum(
                "qhd,khd->hqk", grad_part, values3, preferred_element_type=jnp.float32
            )
            center = jnp.sum(grad_probs * probs, axis=-1, keepdims=True)
            grad_scores = (probs * (grad_probs - center)).astype(jnp.bfloat16)
            grad_keys_acc = (
                grad_keys_acc
                + jnp.einsum(
                    "hqk,qhd->khd", grad_scores, q_part, preferred_element_type=jnp.float32
                )
                * scale
            )
            grad_query = (
                jnp.einsum("hqk,khd->qhd", grad_scores, keys3, preferred_element_type=jnp.float32)
                * scale
            )
            return ((grad_keys_acc, grad_values_acc), grad_query)

        empty_keys = jnp.zeros((group_rows, head_count, HEAD), jnp.float32)
        (grad_keys, grad_values), grad_queries = lax.scan(
            attend_back, (empty_keys, empty_keys), (block_starts, log_totals)
        )
        own_keys, own_values = (
            lax.psum_scatter(
                grad_keys.reshape(group_rows, head_cols).astype(jnp.bfloat16),
                "row",
                scatter_dimension=0,
                tiled=True,
            ).astype(jnp.float32),
            lax.psum_scatter(
                grad_values.reshape(group_rows, head_cols).astype(jnp.bfloat16),
                "row",
                scatter_dimension=0,
                tiled=True,
            ).astype(jnp.float32),
        )
        grad_projected = jnp.stack(
            [grad_queries.reshape(row_rows, head_cols), own_keys, own_values], axis=1
        ).astype(jnp.bfloat16)
        grad_qkv = jnp.einsum(
            "td,tsf->dsf", normed_all, grad_projected, preferred_element_type=jnp.float32
        )
        grad_qkv_bias = jnp.sum(grad_projected.astype(jnp.float32), axis=0)
        grad_normed = sum_inputs(
            jnp.einsum("tsf,dsf->td", grad_projected, w_qkv, preferred_element_type=jnp.float32)
        )
        back_input, grad_gain_one, grad_bias_one = jax.vjp(normalize, residual, ln1_gain, ln1_bias)[
            1
        ](grad_normed)
        input_rows = grad_middle + back_input
        weight_terms = (grad_qkv, grad_out, grad_fc, grad_proj)
        small_terms = (
            grad_gain_one,
            grad_bias_one,
            grad_qkv_bias,
            grad_out_bias,
            grad_gain_two,
            grad_bias_two,
            grad_fc_bias,
            grad_proj_bias,
        )
        return (
            (add_trees(grads_acc, weight_terms), add_trees(small_acc, small_terms)),
            (output_rows, input_rows),
        )

    grads_init = (
        jnp.zeros((width, 3, head_cols), jnp.float32),
        jnp.zeros((head_cols, width), jnp.float32),
        jnp.zeros((width, ff_local), jnp.float32),
        jnp.zeros((ff_local, width), jnp.float32),
    )
    vector_zero = jnp.zeros((width,), jnp.float32)
    small_init = (
        vector_zero,
        vector_zero,
        jnp.zeros((3, head_cols), jnp.float32),
        vector_zero,
        vector_zero,
        vector_zero,
        jnp.zeros((ff_local,), jnp.float32),
        vector_zero,
    )
    (grads_acc, small_acc), (block_out, input_grad) = lax.scan(
        micro_step, (grads_init, small_init), (tokens, cotangent, branch)
    )
    (
        gain_one,
        bias_one,
        qkv_bias_acc,
        out_bias_acc,
        gain_two,
        bias_two,
        fc_bias_acc,
        proj_bias_acc,
    ) = small_acc
    qv_full = lax.dynamic_update_slice(
        jnp.zeros((2, width), jnp.float32),
        jnp.stack([qkv_bias_acc[0], qkv_bias_acc[2]]),
        (jnp.int32(0), col_index * head_cols),
    )
    fc_full = lax.dynamic_update_slice(
        jnp.zeros((ff_local * col_count,), jnp.float32), fc_bias_acc, (col_index * ff_local,)
    )
    summed = lax.psum(
        (gain_one, bias_one, qv_full, out_bias_acc, gain_two, bias_two, fc_full, proj_bias_acc),
        ("dp", "row", "col"),
    )
    return (
        block_out,
        input_grad,
        summed[0],
        summed[1],
        lax.psum_scatter(
            grads_acc[0].astype(jnp.bfloat16), ("dp", "row"), scatter_dimension=0, tiled=True
        ).astype(jnp.float32),
        summed[2],
        lax.psum_scatter(
            grads_acc[1].astype(jnp.bfloat16), ("dp", "row"), scatter_dimension=1, tiled=True
        ).astype(jnp.float32),
        summed[3],
        summed[4],
        summed[5],
        lax.psum_scatter(
            grads_acc[2].astype(jnp.bfloat16), ("dp", "row"), scatter_dimension=0, tiled=True
        ).astype(jnp.float32),
        summed[6],
        lax.psum_scatter(
            grads_acc[3].astype(jnp.bfloat16), ("dp", "row"), scatter_dimension=1, tiled=True
        ).astype(jnp.float32),
        summed[7],
    )


def solution(mesh):
    placed = (
        P("dp", ("row", "col"), None),
        P("dp", ("row", "col"), None),
        P("dp", None),
        P(),
        P(),
        P("row", None, "col"),
        P(None, "col"),
        P("col", "row"),
        P(),
        P(),
        P(),
        P("row", "col"),
        P("col"),
        P("col", "row"),
        P(),
    )
    return jax.shard_map(
        body,
        mesh=mesh,
        in_specs=placed,
        out_specs=(
            P("dp", ("row", "col"), None),
            P("dp", ("row", "col"), None),
            P(),
            P(),
            P(("dp", "row"), None, "col"),
            P(),
            P("col", ("dp", "row")),
            P(),
            P(),
            P(),
            P(("dp", "row"), "col"),
            P(),
            P("col", ("dp", "row")),
            P(),
        ),
        check_vma=False,
    )
```

profile of v0, /device:TPU:0, one launch (start us, length us, event | category | flops | bytes accessed | tf_op | source)
XLA Modules:
  0.0 2760.7 jit_solution(3911327315650754905)
XLA Ops:
  29.1 30.1 %all-gather.23.cloned.1.call-done = bf16[1024,3,512]{2,0,1:T(8,128)(2,1)} async-done(((bf16[256,3,512]{2,0,1:T(8,128)(2,1)}), bf16[1024,3,512]{2,0,1:T(8,128)(2,1)}) %all-gather.23.cloned.1.call-update) | async-done | bytes 3145744 | tf_op jit(solution)/shard_map/all_gather | solution.py:89
  59.2 36.1 %all-gather.29.cloned.1.call-done = bf16[1024,2048]{1,0:T(8,128)(2,1)} async-done(((bf16[256,2048]{1,0:T(8,128)(2,1)}), bf16[1024,2048]{1,0:T(8,128)(2,1)}) %all-gather.29.cloned.1.call-update) | async-done | bytes 4194320 | tf_op jit(solution)/shard_map/all_gather | solution.py:91
  95.3 36.4 %all-gather.25.cloned.1.call-done = bf16[2048,1024]{1,0:T(8,128)(2,1)} async-done(((bf16[2048,256]{1,0:T(8,128)(2,1)}), bf16[2048,1024]{1,0:T(8,128)(2,1)}) %all-gather.25.cloned.1.call-update) | async-done | bytes 4194320 | tf_op jit(solution)/shard_map/all_gather | solution.py:92
  131.7 2337.8 %while.107 = (s32[]{:T(128)}, f32[1024,3,512]{2,0,1:T(8,128)}, f32[512,1024]{1,0:T(8,128)}, f32[1024,2048]{1,0:T(8,128)}, f32[2048,1024]{1,0:T(8,128)}, /*index=...) while((s32[]{:T(128)}, f32[1024,3,512]{2,0,1:T(8,128)}, ...), condition=%wide.region_32.33_spmd.clone.clone, body=%wide.region_0.32_spmd.clone.clone.sunk | while | flops 54250668032 | bytes 1470284544 | solution.py:260
  138.8 33.2 %all-gather.31.cloned.1.call-done = bf16[1024,1024]{1,0:T(8,128)(2,1)} async-done(((bf16[512,1024]{1,0:T(8,128)(2,1)}), bf16[1024,1024]{1,0:T(8,128)(2,1)}) %all-gather.31.cloned.1.call-update) | async-done | bytes 2097168 | tf_op jit(solution)/shard_map/while/body/eval_jaxpr/all_gather | solution.py:77
  180.2 33.6 %all-gather.33.cloned.1.call-done = bf16[4096,1,512]{0,2,1:T(8,128)(2,1)} async-done(((bf16[1024,1,512]{0,2,1:T(8,128)(2,1)}), bf16[4096,1,512]{0,2,1:T(8,128)(2,1)}) %all-gather.33.cloned.1.call-update) | async-done | bytes 4194320 | tf_op jit(solution)/shard_map/while/body/eval_jaxpr/all_gather | solution.py:114
  213.8 36.0 %all-gather.35.cloned.1.call-done = bf16[4096,1,512]{0,2,1:T(8,128)(2,1)} async-done(((bf16[1024,1,512]{0,2,1:T(8,128)(2,1)}), bf16[4096,1,512]{0,2,1:T(8,128)(2,1)}) %all-gather.35.cloned.1.call-update) | async-done | bytes 4194320 | tf_op jit(solution)/shard_map/while/body/eval_jaxpr/all_gather | solution.py:115
  251.0 166.1 %while.108 = (s32[]{:T(128)}, bf16[2,512,8,64]{1,3,2,0:T(8,128)(2,1)}, f32[2,8,512]{2,1,0:T(8,128)S(1)}, s32[4096]{0:T(1024)S(1)}, s32[2]{0:T(128)S(1)}, /*index...) while((s32[]{:T(128)}, ...), condition=%wide.region_7.7_spmd.clone, body=%wide.region_3.6_spmd.clone.sunk | while | flops 4511079424 | bytes 219897072 | solution.py:132
  306.0 27.8 %fusion.204 = bf16[2,512,8,64]{1,3,2,0:T(8,128)(2,1)} fusion(bf16[2,512,8,64]{1,3,2,0:T(8,128)(2,1)} %get-tuple-element.1847, s32[]{:T(128)S(6)} %copy.76, bf16[4096,8,64]{0,2,1:T(8,128)(2,1)} %get-tuple-element.1868, f32[8,512,4096]{2,1,0:T(8,128)} %get-tuple-element.1812, f32[8,512]{1,0:T(8,128)S(1)} %fusion.203, ...), kind=kOutput, calls=%fused_computation.10.clone.1 | convolution fusion | flops 2231369728 | bytes 74481664 | tf_op jit(solution)/shard_map/while/body/eval_jaxpr/while/body/eval_jaxpr/hqk,khd->qhd/dot_general | solution.py:127
  388.8 27.8 %fusion.204 = bf16[2,512,8,64]{1,3,2,0:T(8,128)(2,1)} fusion(bf16[2,512,8,64]{1,3,2,0:T(8,128)(2,1)} %get-tuple-element.1847, s32[]{:T(128)S(6)} %copy.76, bf16[4096,8,64]{0,2,1:T(8,128)(2,1)} %get-tuple-element.1868, f32[8,512,4096]{2,1,0:T(8,128)} %get-tuple-element.1812, f32[8,512]{1,0:T(8,128)S(1)} %fusion.203, ...), kind=kOutput, calls=%fused_computation.10.clone.1 | convolution fusion | flops 2231369728 | bytes 74481664 | tf_op jit(solution)/shard_map/while/body/eval_jaxpr/while/body/eval_jaxpr/hqk,khd->qhd/dot_general | solution.py:127
  424.1 54.5 %reduce-scatter.19.cloned.1.call-done = f32[512,1024]{1,0:T(8,128)} async-done(((f32[1024,1024]{1,0:T(8,128)}), f32[512,1024]{1,0:T(8,128)}) %reduce-scatter.19.cloned.1.call-update) | async-done | bytes 2097168 | tf_op jit(solution)/shard_map/while/body/eval_jaxpr/reduce_scatter | solution.py:83
  485.7 30.1 %all-gather.37.cloned.1.call-done = bf16[1024,1024]{1,0:T(8,128)(2,1)} async-done(((bf16[512,1024]{1,0:T(8,128)(2,1)}), bf16[1024,1024]{1,0:T(8,128)(2,1)}) %all-gather.37.cloned.1.call-update) | async-done | bytes 2097168 | tf_op jit(solution)/shard_map/while/body/eval_jaxpr/all_gather | solution.py:77
  572.4 54.5 %reduce-scatter.21.cloned.1.call-done = f32[512,1024]{1,0:T(8,128)} async-done(((f32[1024,1024]{1,0:T(8,128)}), f32[512,1024]{1,0:T(8,128)}) %reduce-scatter.21.cloned.1.call-update) | async-done | bytes 2097168 | tf_op jit(solution)/shard_map/while/body/eval_jaxpr/reduce_scatter | solution.py:86
  634.2 33.2 %all-gather.41.cloned.1.call-done = bf16[1024,1024]{1,0:T(8,128)(2,1)} async-done(((bf16[512,1024]{1,0:T(8,128)(2,1)}), bf16[1024,1024]{1,0:T(8,128)(2,1)}) %all-gather.41.cloned.1.call-update) | async-done | bytes 2097168 | tf_op jit(solution)/shard_map/while/body/eval_jaxpr/all_gather | solution.py:80
  672.4 396.0 %while.109 = (s32[]{:T(128)}, f32[4096,8,64]{0,2,1:T(8,128)}, f32[4096,8,64]{0,2,1:T(8,128)}, bf16[2,512,8,64]{1,3,2,0:T(8,128)(2,1)}, s32[2]{0:T(128)S(1)}, /*i...) while((s32[]{:T(128)}, f32[4096,8,64]{0,2,1:T(8,128)}, ...), condition=%wide.region_17.17_spmd.clone.clone, body=%wide.region_14.16_spmd.clone.clone.sunk | while | flops 10913946624 | bytes 590913280 | solution.py:196
  679.8 28.7 %subtract_exponential_fusion.3 = f32[8,512,4096]{2,1,0:T(8,128)} fusion(bf16[4096,8,64]{0,2,1:T(8,128)(2,1)} %get-tuple-element.1913, f32[8,512]{1,0:T(8,128)S(1)} %dynamic-slice_bitcast_fusion.2, pred[512,4096]{1,0:T(8,128)(4,1)S(1)} %and_or_fusion.5, bf16[1024,8,64]{0,2,1:T(8,128)(2,1)S(1)} %get-tuple-element.1909, s32[]{:T(128)S(6)} %select_n.260), kind=kOutput, calls=%fused_computation.40.clone.1 | convolution fusion | flops 2197815296 | bytes 73940992 | tf_op jit(solution)/shard_map/while/body/eval_jaxpr/while/body/eval_jaxpr/qhd,khd->hqk/dot_general | solution.py:100
  734.5 43.6 %multiply_reduce_fusion.9 = (f32[8,512]{1,0:T(8,128)S(1)}, f32[8,512,4096]{2,1,0:T(8,128)}) fusion(f32[8,512,4096]{2,1,0:T(8,128)} %subtract_exponential_fusion.3, bf16[4096,8,64]{0,2,1:T(8,128)(2,1)S(1)} %copy-done, bf16[1024,8,64]{0,2,1:T(8,128)(2,1)} %get-tuple-element.1915, s32[]{:T(128)S(6)} %select_n.260), kind=kOutput, calls=%fused_computation.39.clone.2 | convolution fusion | flops 2181033984 | bytes 138952704 | tf_op jit(solution)/shard_map/while/body/eval_jaxpr/while/body/eval_jaxpr/qhd,khd->hqk/dot_general | solution.py:177
  778.1 53.0 %multiply_convert_fusion.9 = bf16[8,512,4096]{2,1,0:T(8,128)(2,1)} fusion(f32[8,512,4096]{2,1,0:T(8,128)} %subtract_exponential_fusion.3, f32[8,512,4096]{2,1,0:T(8,128)} %get-tuple-element.1831, f32[8,512]{1,0:T(8,128)S(1)} %get-tuple-element.1832), kind=kLoop, calls=%fused_computation.38.clone.1 | loop fusion | flops 50331648 | bytes 167788544 | tf_op jit(solution)/shard_map/while/body/eval_jaxpr/while/body/eval_jaxpr/convert_element_type | solution.py:181
  875.2 28.7 %subtract_exponential_fusion.3 = f32[8,512,4096]{2,1,0:T(8,128)} fusion(bf16[4096,8,64]{0,2,1:T(8,128)(2,1)} %get-tuple-element.1913, f32[8,512]{1,0:T(8,128)S(1)} %dynamic-slice_bitcast_fusion.2, pred[512,4096]{1,0:T(8,128)(4,1)S(1)} %and_or_fusion.5, bf16[1024,8,64]{0,2,1:T(8,128)(2,1)S(1)} %get-tuple-element.1909, s32[]{:T(128)S(6)} %select_n.260), kind=kOutput, calls=%fused_computation.40.clone.1 | convolution fusion | flops 2197815296 | bytes 73940992 | tf_op jit(solution)/shard_map/while/body/eval_jaxpr/while/body/eval_jaxpr/qhd,khd->hqk/dot_general | solution.py:100
  903.9 28.3 %bitcast_add_fusion.5 = f32[4096,8,64]{0,2,1:T(8,128)} fusion(f32[4096,8,64]{0,2,1:T(8,128)} %get-tuple-element.1890, f32[8,512,4096]{2,1,0:T(8,128)} %subtract_exponential_fusion.3, pred[]{:T(512)S(6)} %compare.79, bf16[1024,8,64]{0,2,1:T(8,128)(2,1)} %get-tuple-element.1915, s32[]{:T(128)S(6)} %select_n.260), kind=kOutput, calls=%fused_computation.43.clone.1 | convolution fusion | flops 2168455168 | bytes 84410376 | tf_op jit(solution)/shard_map/while/body/eval_jaxpr/while/body/eval_jaxpr/hqk,qhd->khd/dot_general | solution.py:174
  932.2 43.6 %multiply_reduce_fusion.9 = (f32[8,512]{1,0:T(8,128)S(1)}, f32[8,512,4096]{2,1,0:T(8,128)}) fusion(f32[8,512,4096]{2,1,0:T(8,128)} %subtract_exponential_fusion.3, bf16[4096,8,64]{0,2,1:T(8,128)(2,1)S(1)} %copy-done, bf16[1024,8,64]{0,2,1:T(8,128)(2,1)} %get-tuple-element.1915, s32[]{:T(128)S(6)} %select_n.260), kind=kOutput, calls=%fused_computation.39.clone.2 | convolution fusion | flops 2181033984 | bytes 138952704 | tf_op jit(solution)/shard_map/while/body/eval_jaxpr/while/body/eval_jaxpr/qhd,khd->hqk/dot_general | solution.py:177
  975.8 53.0 %multiply_convert_fusion.9 = bf16[8,512,4096]{2,1,0:T(8,128)(2,1)} fusion(f32[8,512,4096]{2,1,0:T(8,128)} %subtract_exponential_fusion.3, f32[8,512,4096]{2,1,0:T(8,128)} %get-tuple-element.1831, f32[8,512]{1,0:T(8,128)S(1)} %get-tuple-element.1832), kind=kLoop, calls=%fused_computation.38.clone.1 | loop fusion | flops 50331648 | bytes 167788544 | tf_op jit(solution)/shard_map/while/body/eval_jaxpr/while/body/eval_jaxpr/convert_element_type | solution.py:181
  1125.6 47.0 %reduce-scatter.23.cloned.1.call-done = bf16[1024,512]{1,0:T(8,128)(2,1)} async-done(((bf16[4096,512]{1,0:T(8,128)(2,1)}), bf16[1024,512]{1,0:T(8,128)(2,1)}) %reduce-scatter.23.cloned.1.call-update) | async-done | bytes 1048592 | tf_op jit(solution)/shard_map/while/body/eval_jaxpr/reduce_scatter | solution.py:206
  1241.5 44.2 %reduce-scatter.27.cloned.1.call-done = f32[512,1024]{1,0:T(8,128)} async-done(((f32[1024,1024]{1,0:T(8,128)}), f32[512,1024]{1,0:T(8,128)}) %reduce-scatter.27.cloned.1.call-update) | async-done | bytes 2097168 | tf_op jit(solution)/shard_map/while/body/eval_jaxpr/reduce_scatter | solution.py:86
  1300.4 33.2 %all-gather.31.cloned.1.call-done = bf16[1024,1024]{1,0:T(8,128)(2,1)} async-done(((bf16[512,1024]{1,0:T(8,128)(2,1)}), bf16[1024,1024]{1,0:T(8,128)(2,1)}) %all-gather.31.cloned.1.call-update) | async-done | bytes 2097168 | tf_op jit(solution)/shard_map/while/body/eval_jaxpr/all_gather | solution.py:77
  1342.0 33.4 %all-gather.33.cloned.1.call-done = bf16[4096,1,512]{0,2,1:T(8,128)(2,1)} async-done(((bf16[1024,1,512]{0,2,1:T(8,128)(2,1)}), bf16[4096,1,512]{0,2,1:T(8,128)(2,1)}) %all-gather.33.cloned.1.call-update) | async-done | bytes 4194320 | tf_op jit(solution)/shard_map/while/body/eval_jaxpr/all_gather | solution.py:114
  1375.4 36.0 %all-gather.35.cloned.1.call-done = bf16[4096,1,512]{0,2,1:T(8,128)(2,1)} async-done(((bf16[1024,1,512]{0,2,1:T(8,128)(2,1)}), bf16[4096,1,512]{0,2,1:T(8,128)(2,1)}) %all-gather.35.cloned.1.call-update) | async-done | bytes 4194320 | tf_op jit(solution)/shard_map/while/body/eval_jaxpr/all_gather | solution.py:115
  1412.5 177.5 %while.108 = (s32[]{:T(128)}, bf16[2,512,8,64]{1,3,2,0:T(8,128)(2,1)}, f32[2,8,512]{2,1,0:T(8,128)S(1)}, s32[4096]{0:T(1024)S(1)}, s32[2]{0:T(128)S(1)}, /*index...) while((s32[]{:T(128)}, ...), condition=%wide.region_7.7_spmd.clone, body=%wide.region_3.6_spmd.clone.sunk | while | flops 4511079424 | bytes 219897072 | solution.py:132
  1467.5 27.8 %fusion.204 = bf16[2,512,8,64]{1,3,2,0:T(8,128)(2,1)} fusion(bf16[2,512,8,64]{1,3,2,0:T(8,128)(2,1)} %get-tuple-element.1847, s32[]{:T(128)S(6)} %copy.76, bf16[4096,8,64]{0,2,1:T(8,128)(2,1)} %get-tuple-element.1868, f32[8,512,4096]{2,1,0:T(8,128)} %get-tuple-element.1812, f32[8,512]{1,0:T(8,128)S(1)} %fusion.203, ...), kind=kOutput, calls=%fused_computation.10.clone.1 | convolution fusion | flops 2231369728 | bytes 74481664 | tf_op jit(solution)/shard_map/while/body/eval_jaxpr/while/body/eval_jaxpr/hqk,khd->qhd/dot_general | solution.py:127
  1550.4 27.8 %fusion.204 = bf16[2,512,8,64]{1,3,2,0:T(8,128)(2,1)} fusion(bf16[2,512,8,64]{1,3,2,0:T(8,128)(2,1)} %get-tuple-element.1847, s32[]{:T(128)S(6)} %copy.76, bf16[4096,8,64]{0,2,1:T(8,128)(2,1)} %get-tuple-element.1868, f32[8,512,4096]{2,1,0:T(8,128)} %get-tuple-element.1812, f32[8,512]{1,0:T(8,128)S(1)} %fusion.203, ...), kind=kOutput, calls=%fused_computation.10.clone.1 | convolution fusion | flops 2231369728 | bytes 74481664 | tf_op jit(solution)/shard_map/while/body/eval_jaxpr/while/body/eval_jaxpr/hqk,khd->qhd/dot_general | solution.py:127
  1597.1 54.5 %reduce-scatter.19.cloned.1.call-done = f32[512,1024]{1,0:T(8,128)} async-done(((f32[1024,1024]{1,0:T(8,128)}), f32[512,1024]{1,0:T(8,128)}) %reduce-scatter.19.cloned.1.call-update) | async-done | bytes 2097168 | tf_op jit(solution)/shard_map/while/body/eval_jaxpr/reduce_scatter | solution.py:83
  1658.7 30.1 %all-gather.37.cloned.1.call-done = bf16[1024,1024]{1,0:T(8,128)(2,1)} async-done(((bf16[512,1024]{1,0:T(8,128)(2,1)}), bf16[1024,1024]{1,0:T(8,128)(2,1)}) %all-gather.37.cloned.1.call-update) | async-done | bytes 2097168 | tf_op jit(solution)/shard_map/while/body/eval_jaxpr/all_gather | solution.py:77
  1745.5 54.5 %reduce-scatter.21.cloned.1.call-done = f32[512,1024]{1,0:T(8,128)} async-done(((f32[1024,1024]{1,0:T(8,128)}), f32[512,1024]{1,0:T(8,128)}) %reduce-scatter.21.cloned.1.call-update) | async-done | bytes 2097168 | tf_op jit(solution)/shard_map/while/body/eval_jaxpr/reduce_scatter | solution.py:86
  1807.3 33.2 %all-gather.41.cloned.1.call-done = bf16[1024,1024]{1,0:T(8,128)(2,1)} async-done(((bf16[512,1024]{1,0:T(8,128)(2,1)}), bf16[1024,1024]{1,0:T(8,128)(2,1)}) %all-gather.41.cloned.1.call-update) | async-done | bytes 2097168 | tf_op jit(solution)/shard_map/while/body/eval_jaxpr/all_gather | solution.py:80
  1845.5 396.0 %while.109 = (s32[]{:T(128)}, f32[4096,8,64]{0,2,1:T(8,128)}, f32[4096,8,64]{0,2,1:T(8,128)}, bf16[2,512,8,64]{1,3,2,0:T(8,128)(2,1)}, s32[2]{0:T(128)S(1)}, /*i...) while((s32[]{:T(128)}, f32[4096,8,64]{0,2,1:T(8,128)}, ...), condition=%wide.region_17.17_spmd.clone.clone, body=%wide.region_14.16_spmd.clone.clone.sunk | while | flops 10913946624 | bytes 590913280 | solution.py:196
  1853.1 28.7 %subtract_exponential_fusion.3 = f32[8,512,4096]{2,1,0:T(8,128)} fusion(bf16[4096,8,64]{0,2,1:T(8,128)(2,1)} %get-tuple-element.1913, f32[8,512]{1,0:T(8,128)S(1)} %dynamic-slice_bitcast_fusion.2, pred[512,4096]{1,0:T(8,128)(4,1)S(1)} %and_or_fusion.5, bf16[1024,8,64]{0,2,1:T(8,128)(2,1)S(1)} %get-tuple-element.1909, s32[]{:T(128)S(6)} %select_n.260), kind=kOutput, calls=%fused_computation.40.clone.1 | convolution fusion | flops 2197815296 | bytes 73940992 | tf_op jit(solution)/shard_map/while/body/eval_jaxpr/while/body/eval_jaxpr/qhd,khd->hqk/dot_general | solution.py:100
  1907.8 43.6 %multiply_reduce_fusion.9 = (f32[8,512]{1,0:T(8,128)S(1)}, f32[8,512,4096]{2,1,0:T(8,128)}) fusion(f32[8,512,4096]{2,1,0:T(8,128)} %subtract_exponential_fusion.3, bf16[4096,8,64]{0,2,1:T(8,128)(2,1)S(1)} %copy-done, bf16[1024,8,64]{0,2,1:T(8,128)(2,1)} %get-tuple-element.1915, s32[]{:T(128)S(6)} %select_n.260), kind=kOutput, calls=%fused_computation.39.clone.2 | convolution fusion | flops 2181033984 | bytes 138952704 | tf_op jit(solution)/shard_map/while/body/eval_jaxpr/while/body/eval_jaxpr/qhd,khd->hqk/dot_general | solution.py:177
  1951.4 53.0 %multiply_convert_fusion.9 = bf16[8,512,4096]{2,1,0:T(8,128)(2,1)} fusion(f32[8,512,4096]{2,1,0:T(8,128)} %subtract_exponential_fusion.3, f32[8,512,4096]{2,1,0:T(8,128)} %get-tuple-element.1831, f32[8,512]{1,0:T(8,128)S(1)} %get-tuple-element.1832), kind=kLoop, calls=%fused_computation.38.clone.1 | loop fusion | flops 50331648 | bytes 167788544 | tf_op jit(solution)/shard_map/while/body/eval_jaxpr/while/body/eval_jaxpr/convert_element_type | solution.py:181
  2048.5 28.7 %subtract_exponential_fusion.3 = f32[8,512,4096]{2,1,0:T(8,128)} fusion(bf16[4096,8,64]{0,2,1:T(8,128)(2,1)} %get-tuple-element.1913, f32[8,512]{1,0:T(8,128)S(1)} %dynamic-slice_bitcast_fusion.2, pred[512,4096]{1,0:T(8,128)(4,1)S(1)} %and_or_fusion.5, bf16[1024,8,64]{0,2,1:T(8,128)(2,1)S(1)} %get-tuple-element.1909, s32[]{:T(128)S(6)} %select_n.260), kind=kOutput, calls=%fused_computation.40.clone.1 | convolution fusion | flops 2197815296 | bytes 73940992 | tf_op jit(solution)/shard_map/while/body/eval_jaxpr/while/body/eval_jaxpr/qhd,khd->hqk/dot_general | solution.py:100
  2077.2 28.3 %bitcast_add_fusion.5 = f32[4096,8,64]{0,2,1:T(8,128)} fusion(f32[4096,8,64]{0,2,1:T(8,128)} %get-tuple-element.1890, f32[8,512,4096]{2,1,0:T(8,128)} %subtract_exponential_fusion.3, pred[]{:T(512)S(6)} %compare.79, bf16[1024,8,64]{0,2,1:T(8,128)(2,1)} %get-tuple-element.1915, s32[]{:T(128)S(6)} %select_n.260), kind=kOutput, calls=%fused_computation.43.clone.1 | convolution fusion | flops 2168455168 | bytes 84410376 | tf_op jit(solution)/shard_map/while/body/eval_jaxpr/while/body/eval_jaxpr/hqk,qhd->khd/dot_general | solution.py:174
  2105.6 43.6 %multiply_reduce_fusion.9 = (f32[8,512]{1,0:T(8,128)S(1)}, f32[8,512,4096]{2,1,0:T(8,128)}) fusion(f32[8,512,4096]{2,1,0:T(8,128)} %subtract_exponential_fusion.3, bf16[4096,8,64]{0,2,1:T(8,128)(2,1)S(1)} %copy-done, bf16[1024,8,64]{0,2,1:T(8,128)(2,1)} %get-tuple-element.1915, s32[]{:T(128)S(6)} %select_n.260), kind=kOutput, calls=%fused_computation.39.clone.2 | convolution fusion | flops 2181033984 | bytes 138952704 | tf_op jit(solution)/shard_map/while/body/eval_jaxpr/while/body/eval_jaxpr/qhd,khd->hqk/dot_general | solution.py:177
  2149.1 53.0 %multiply_convert_fusion.9 = bf16[8,512,4096]{2,1,0:T(8,128)(2,1)} fusion(f32[8,512,4096]{2,1,0:T(8,128)} %subtract_exponential_fusion.3, f32[8,512,4096]{2,1,0:T(8,128)} %get-tuple-element.1831, f32[8,512]{1,0:T(8,128)S(1)} %get-tuple-element.1832), kind=kLoop, calls=%fused_computation.38.clone.1 | loop fusion | flops 50331648 | bytes 167788544 | tf_op jit(solution)/shard_map/while/body/eval_jaxpr/while/body/eval_jaxpr/convert_element_type | solution.py:181
  2298.7 47.0 %reduce-scatter.23.cloned.1.call-done = bf16[1024,512]{1,0:T(8,128)(2,1)} async-done(((bf16[4096,512]{1,0:T(8,128)(2,1)}), bf16[1024,512]{1,0:T(8,128)(2,1)}) %reduce-scatter.23.cloned.1.call-update) | async-done | bytes 1048592 | tf_op jit(solution)/shard_map/while/body/eval_jaxpr/reduce_scatter | solution.py:206
  2416.9 42.1 %reduce-scatter.27.cloned.1.call-done = f32[512,1024]{1,0:T(8,128)} async-done(((f32[1024,1024]{1,0:T(8,128)}), f32[512,1024]{1,0:T(8,128)}) %reduce-scatter.27.cloned.1.call-update) | async-done | bytes 2097168 | tf_op jit(solution)/shard_map/while/body/eval_jaxpr/reduce_scatter | solution.py:86
  2491.7 40.9 %all-reduce = (f32[1024]{0:T(1024)}, f32[1024]{0:T(1024)}, f32[2,1024]{1,0:T(2,128)}, f32[1024]{0:T(1024)}, f32[1024]{0:T(1024)}, /*index=5*/f32[1024]{0:T(1024)}, f32[4096]{0:T(1024)}, f32[1024]{0:T(1024)}) all-reduce(f32[1024]{0:T(1024)S(1)} %copy-done.69, ...), channel_id=1, replica_groups=mesh['dp'=4,'row'=4,'col'=2] {'dp','row','col'}, use_global_device_ids=true, to_apply=%region_33.34 | all-reduce | flops 12288 | bytes 98304 | tf_op jit(solution)/shard_map/psum | solution.py:281
  2534.1 66.8 %reduce-scatter.11.cloned.1.call-done = bf16[64,3,512]{2,0,1:T(8,128)(2,1)} async-done(((bf16[1024,3,512]{2,0,1:T(8,128)(2,1)}), bf16[64,3,512]{2,0,1:T(8,128)(2,1)}) %reduce-scatter.11.cloned.1.call-update) | async-done | bytes 196624 | tf_op jit(solution)/shard_map/reduce_scatter | solution.py:290
  2602.6 73.7 %reduce-scatter.15.cloned.1.call-done = bf16[64,2048]{1,0:T(8,128)(2,1)} async-done(((bf16[1024,2048]{1,0:T(8,128)(2,1)}), bf16[64,2048]{1,0:T(8,128)(2,1)}) %reduce-scatter.15.cloned.1.call-update) | async-done | bytes 262160 | tf_op jit(solution)/shard_map/reduce_scatter | solution.py:300
  2678.2 73.9 %reduce-scatter.17.cloned.1.call-done = bf16[2048,64]{0,1:T(8,128)(2,1)} async-done(((bf16[2048,1024]{0,1:T(8,128)(2,1)}), bf16[2048,64]{0,1:T(8,128)(2,1)}) %reduce-scatter.17.cloned.1.call-update) | async-done | bytes 262160 | tf_op jit(solution)/shard_map/reduce_scatter | solution.py:304
  (668 shorter events, 949.3 us)
Async XLA Ops:
  7.2 21.9 all-gather.27.cloned.1.call-start
  7.9 51.3 %all-gather.23.cloned.1.call-start = ((), (), s32[]{:S(2)}) async-start(), calls=%async_computation.10 | async-start | bytes 3932160 | tf_op jit(solution)/shard_map/all_gather | solution.py:89
  8.7 86.6 %all-gather.29.cloned.1.call-start = ((), (), s32[]{:S(2)}) async-start(), calls=%async_computation.13 | async-start | bytes 5242880 | tf_op jit(solution)/shard_map/all_gather | solution.py:91
  9.4 122.3 %all-gather.25.cloned.1.call-start = ((), (), s32[]{:S(2)}) async-start(), calls=%async_computation.11 | async-start | bytes 5242880 | tf_op jit(solution)/shard_map/all_gather | solution.py:92
  131.7 40.3 %all-gather.31.cloned.1.call-start = ((), (), s32[]{:S(2)}) async-start(), calls=%async_computation.18 | async-start | bytes 3145728 | tf_op jit(solution)/shard_map/while/body/eval_jaxpr/all_gather | solution.py:77
  138.8 75.0 %all-gather.33.cloned.1.call-start = ((), (), s32[]{:S(2)}) async-start(), calls=%async_computation.19 | async-start | bytes 5242880 | tf_op jit(solution)/shard_map/while/body/eval_jaxpr/all_gather | solution.py:114
  179.2 70.7 %all-gather.35.cloned.1.call-start = ((), (), s32[]{:S(2)}) async-start(), calls=%async_computation.20 | async-start | bytes 5242880 | tf_op jit(solution)/shard_map/while/body/eval_jaxpr/all_gather | solution.py:115
  179.9 298.6 %reduce-scatter.19.cloned.1.call-start = ((), (), s32[]{:S(2)}) async-start(), calls=%async_computation.21 | async-start | bytes 6291456 | tf_op jit(solution)/shard_map/while/body/eval_jaxpr/reduce_scatter | solution.py:83
  420.7 57.9 %copy-start.72 = (f32[1024]{0:T(1024)S(1)}, f32[1024]{0:T(1024)}, u32[]{:S(2)}) copy-start(f32[1024]{0:T(1024)} %get-tuple-element.2025) | copy-start | bytes 12292 | tf_op jit(solution)/shard_map/while
  424.0 57.1 %copy-start.34 = (f32[1024]{0:T(1024)S(1)}, f32[1024]{0:T(1024)}, u32[]{:S(2)}) copy-start(f32[1024]{0:T(1024)} %get-tuple-element.2026) | copy-start | bytes 12292 | tf_op jit(solution)/shard_map/while
  424.1 57.1 %copy-start.70 = (f32[1024]{0:T(1024)S(1)}, f32[1024]{0:T(1024)}, u32[]{:S(2)}) copy-start(f32[1024]{0:T(1024)} %get-tuple-element.2027) | copy-start | bytes 12292 | tf_op jit(solution)/shard_map/while
  424.1 91.8 %all-gather.37.cloned.1.call-start = ((), (), s32[]{:S(2)}) async-start(), calls=%async_computation.22 | async-start | bytes 3145728 | tf_op jit(solution)/shard_map/while/body/eval_jaxpr/all_gather | solution.py:77
  480.8 149.2 %copy-start.1 = (f32[512,1024]{1,0:T(8,128)}, f32[512,1024]{1,0:T(8,128)S(1)}, u32[]{:S(2)}) copy-start(f32[512,1024]{1,0:T(8,128)S(1)} %get-tuple-element.1774) | copy-start | bytes 6291460 | tf_op jit(solution)/shard_map/while
  482.6 67.8 %all-gather.39.cloned.1.call-start = ((), (), s32[]{:S(2)}) async-start(), calls=%async_computation.23 | async-start | bytes 3145728 | tf_op jit(solution)/shard_map/while/body/eval_jaxpr/all_gather | solution.py:80
  485.7 141.2 %reduce-scatter.21.cloned.1.call-start = ((), (), s32[]{:S(2)}) async-start(), calls=%async_computation.24 | async-start | bytes 6291456 | tf_op jit(solution)/shard_map/while/body/eval_jaxpr/reduce_scatter | solution.py:86
  572.4 95.0 %all-gather.41.cloned.1.call-start = ((), (), s32[]{:S(2)}) async-start(), calls=%async_computation.25 | async-start | bytes 3145728 | tf_op jit(solution)/shard_map/while/body/eval_jaxpr/all_gather | solution.py:80
  634.1 491.5 %reduce-scatter.25.cloned.1.call-start = ((), (), s32[]{:S(2)}) async-start(), calls=%async_computation.27 | async-start | bytes 5242880 | tf_op jit(solution)/shard_map/while/body/eval_jaxpr/reduce_scatter | solution.py:200
  778.1 53.0 %copy-start.18 = (bf16[2,512,8,64]{1,3,2,0:T(8,128)(2,1)S(1)}, bf16[2,512,8,64]{1,3,2,0:T(8,128)(2,1)}, u32[]{:S(2)}) copy-start(bf16[2,512,8,64]{1,3,2,0:T(8,128)(2,1)} %get-tuple-element.1891) | copy-start | bytes 3145732 | tf_op jit(solution)/shard_map/while/body/eval_jaxpr/while
  975.8 53.0 %copy-start.18 = (bf16[2,512,8,64]{1,3,2,0:T(8,128)(2,1)S(1)}, bf16[2,512,8,64]{1,3,2,0:T(8,128)(2,1)}, u32[]{:S(2)}) copy-start(bf16[2,512,8,64]{1,3,2,0:T(8,128)(2,1)} %get-tuple-element.1891) | copy-start | bytes 3145732 | tf_op jit(solution)/shard_map/while/body/eval_jaxpr/while
  1080.9 91.7 %reduce-scatter.23.cloned.1.call-start = ((), (), s32[]{:S(2)}) async-start(), calls=%async_computation.26 | async-start | bytes 5242880 | tf_op jit(solution)/shard_map/while/body/eval_jaxpr/reduce_scatter | solution.py:206
  1093.8 135.4 %reduce-scatter.29.cloned.1.call-start = ((), (), s32[]{:S(2)}) async-start(), calls=%async_computation.29 | async-start | bytes 6291456 | tf_op jit(solution)/shard_map/while/body/eval_jaxpr/reduce_scatter | solution.py:83
  1106.4 179.4 %reduce-scatter.27.cloned.1.call-start = ((), (), s32[]{:S(2)}) async-start(), calls=%async_computation.28 | async-start | bytes 6291456 | tf_op jit(solution)/shard_map/while/body/eval_jaxpr/reduce_scatter | solution.py:86
  1110.5 70.1 %copy-start.16 = (bf16[1024,1,512]{2,0,1:T(8,128)(2,1)}, bf16[1024,1,512]{2,0,1:T(8,128)(2,1)S(1)}, u32[]{:S(2)}) copy-start(bf16[1024,1,512]{2,0,1:T(8,128)(2,1)S(1)} %reshape.542) | copy-start | bytes 3145732 | tf_op jit(solution)/shard_map/while
  1293.2 40.4 %all-gather.31.cloned.1.call-start = ((), (), s32[]{:S(2)}) async-start(), calls=%async_computation.18 | async-start | bytes 3145728 | tf_op jit(solution)/shard_map/while/body/eval_jaxpr/all_gather | solution.py:77
  1300.4 75.0 %all-gather.33.cloned.1.call-start = ((), (), s32[]{:S(2)}) async-start(), calls=%async_computation.19 | async-start | bytes 5242880 | tf_op jit(solution)/shard_map/while/body/eval_jaxpr/all_gather | solution.py:114
  1340.7 70.7 %all-gather.35.cloned.1.call-start = ((), (), s32[]{:S(2)}) async-start(), calls=%async_computation.20 | async-start | bytes 5242880 | tf_op jit(solution)/shard_map/while/body/eval_jaxpr/all_gather | solution.py:115
  1341.5 310.0 %reduce-scatter.19.cloned.1.call-start = ((), (), s32[]{:S(2)}) async-start(), calls=%async_computation.21 | async-start | bytes 6291456 | tf_op jit(solution)/shard_map/while/body/eval_jaxpr/reduce_scatter | solution.py:83
  1593.7 57.9 %copy-start.72 = (f32[1024]{0:T(1024)S(1)}, f32[1024]{0:T(1024)}, u32[]{:S(2)}) copy-start(f32[1024]{0:T(1024)} %get-tuple-element.2025) | copy-start | bytes 12292 | tf_op jit(solution)/shard_map/while
  1597.0 57.1 %copy-start.34 = (f32[1024]{0:T(1024)S(1)}, f32[1024]{0:T(1024)}, u32[]{:S(2)}) copy-start(f32[1024]{0:T(1024)} %get-tuple-element.2026) | copy-start | bytes 12292 | tf_op jit(solution)/shard_map/while
  1597.0 57.1 %copy-start.70 = (f32[1024]{0:T(1024)S(1)}, f32[1024]{0:T(1024)}, u32[]{:S(2)}) copy-start(f32[1024]{0:T(1024)} %get-tuple-element.2027) | copy-start | bytes 12292 | tf_op jit(solution)/shard_map/while
  1597.0 91.8 %all-gather.37.cloned.1.call-start = ((), (), s32[]{:S(2)}) async-start(), calls=%async_computation.22 | async-start | bytes 3145728 | tf_op jit(solution)/shard_map/while/body/eval_jaxpr/all_gather | solution.py:77
  1653.8 149.4 %copy-start.1 = (f32[512,1024]{1,0:T(8,128)}, f32[512,1024]{1,0:T(8,128)S(1)}, u32[]{:S(2)}) copy-start(f32[512,1024]{1,0:T(8,128)S(1)} %get-tuple-element.1774) | copy-start | bytes 6291460 | tf_op jit(solution)/shard_map/while
  1655.5 67.9 %all-gather.39.cloned.1.call-start = ((), (), s32[]{:S(2)}) async-start(), calls=%async_computation.23 | async-start | bytes 3145728 | tf_op jit(solution)/shard_map/while/body/eval_jaxpr/all_gather | solution.py:80
  1658.6 141.4 %reduce-scatter.21.cloned.1.call-start = ((), (), s32[]{:S(2)}) async-start(), calls=%async_computation.24 | async-start | bytes 6291456 | tf_op jit(solution)/shard_map/while/body/eval_jaxpr/reduce_scatter | solution.py:86
  1745.5 95.0 %all-gather.41.cloned.1.call-start = ((), (), s32[]{:S(2)}) async-start(), calls=%async_computation.25 | async-start | bytes 3145728 | tf_op jit(solution)/shard_map/while/body/eval_jaxpr/all_gather | solution.py:80
  1807.2 491.5 %reduce-scatter.25.cloned.1.call-start = ((), (), s32[]{:S(2)}) async-start(), calls=%async_computation.27 | async-start | bytes 5242880 | tf_op jit(solution)/shard_map/while/body/eval_jaxpr/reduce_scatter | solution.py:200
  1951.4 53.0 %copy-start.18 = (bf16[2,512,8,64]{1,3,2,0:T(8,128)(2,1)S(1)}, bf16[2,512,8,64]{1,3,2,0:T(8,128)(2,1)}, u32[]{:S(2)}) copy-start(bf16[2,512,8,64]{1,3,2,0:T(8,128)(2,1)} %get-tuple-element.1891) | copy-start | bytes 3145732 | tf_op jit(solution)/shard_map/while/body/eval_jaxpr/while
  2149.1 53.0 %copy-start.18 = (bf16[2,512,8,64]{1,3,2,0:T(8,128)(2,1)S(1)}, bf16[2,512,8,64]{1,3,2,0:T(8,128)(2,1)}, u32[]{:S(2)}) copy-start(bf16[2,512,8,64]{1,3,2,0:T(8,128)(2,1)} %get-tuple-element.1891) | copy-start | bytes 3145732 | tf_op jit(solution)/shard_map/while/body/eval_jaxpr/while
  2254.0 91.7 %reduce-scatter.23.cloned.1.call-start = ((), (), s32[]{:S(2)}) async-start(), calls=%async_computation.26 | async-start | bytes 5242880 | tf_op jit(solution)/shard_map/while/body/eval_jaxpr/reduce_scatter | solution.py:206
  2266.9 135.4 %reduce-scatter.29.cloned.1.call-start = ((), (), s32[]{:S(2)}) async-start(), calls=%async_computation.29 | async-start | bytes 6291456 | tf_op jit(solution)/shard_map/while/body/eval_jaxpr/reduce_scatter | solution.py:83
  2279.5 179.5 %reduce-scatter.27.cloned.1.call-start = ((), (), s32[]{:S(2)}) async-start(), calls=%async_computation.28 | async-start | bytes 6291456 | tf_op jit(solution)/shard_map/while/body/eval_jaxpr/reduce_scatter | solution.py:86
  2283.6 70.1 %copy-start.16 = (bf16[1024,1,512]{2,0,1:T(8,128)(2,1)}, bf16[1024,1,512]{2,0,1:T(8,128)(2,1)S(1)}, u32[]{:S(2)}) copy-start(bf16[1024,1,512]{2,0,1:T(8,128)(2,1)S(1)} %reshape.542) | copy-start | bytes 3145732 | tf_op jit(solution)/shard_map/while
  2408.7 52.5 %copy-start.40 = (f32[512]{0:T(512)S(1)}, f32[512]{0:T(512)}, u32[]{:S(2)}) copy-start(f32[512]{0:T(512)} %copy-done.39) | copy-start | bytes 6148 | tf_op jit(solution)/shard_map/while
  2408.7 52.5 %copy-start.36 = (f32[512]{0:T(512)S(1)}, f32[512]{0:T(512)}, u32[]{:S(2)}) copy-start(f32[512]{0:T(512)} %copy-done.35) | copy-start | bytes 6148 | tf_op jit(solution)/shard_map/while
  2469.5 63.1 %reduce-scatter.13.cloned.1.call-start = ((), (), s32[]{:S(2)}) async-start(), calls=%async_computation.15 | async-start | bytes 1114112 | tf_op jit(solution)/shard_map/reduce_scatter | solution.py:294
  2472.2 128.7 %reduce-scatter.11.cloned.1.call-start = ((), (), s32[]{:S(2)}) async-start(), calls=%async_computation.14 | async-start | bytes 3342336 | tf_op jit(solution)/shard_map/reduce_scatter | solution.py:290
  2477.1 199.3 %reduce-scatter.15.cloned.1.call-start = ((), (), s32[]{:S(2)}) async-start(), calls=%async_computation.16 | async-start | bytes 4456448 | tf_op jit(solution)/shard_map/reduce_scatter | solution.py:300
  2483.2 268.8 %reduce-scatter.17.cloned.1.call-start = ((), (), s32[]{:S(2)}) async-start(), calls=%async_computation.17 | async-start | bytes 4456448 | tf_op jit(solution)/shard_map/reduce_scatter | solution.py:304
  (172 other events, 3074.6 us)
Sparse Core Ops, SparseCore 0:
  9.5 19.5 all-gather.26
  30.7 28.4 all-gather.22
  60.8 34.4 all-gather.28
  96.7 34.9 all-gather.24
  138.9 33.0 all-gather.30
  179.3 34.4 all-gather.32
  215.3 34.4 all-gather.34
  424.2 54.3 reduce-scatter.18
  482.7 33.0 all-gather.36
  517.2 33.0 all-gather.38
  572.5 54.3 reduce-scatter.20
  634.2 33.0 all-gather.40
  1081.0 44.5 reduce-scatter.24
  1128.0 44.5 reduce-scatter.22
  1174.7 54.3 reduce-scatter.28
  1231.3 54.3 reduce-scatter.26
  1300.5 33.0 all-gather.30
  1340.9 34.4 all-gather.32
  1376.9 34.4 all-gather.34
  1597.1 54.3 reduce-scatter.18
  1655.7 33.0 all-gather.36
  1690.3 33.0 all-gather.38
  1745.6 54.3 reduce-scatter.20
  1807.3 33.0 all-gather.40
  2254.1 44.5 reduce-scatter.24
  2301.1 44.5 reduce-scatter.22
  2347.9 54.3 reduce-scatter.28
  2404.6 54.3 reduce-scatter.26
  2474.0 57.7 reduce-scatter.12
  2535.4 65.4 reduce-scatter.10
  2604.8 71.5 reduce-scatter.14
  2680.2 71.7 reduce-scatter.16
where the time goes:
time: 2770 us; the launch traced here: 2760 us
  waiting for transfers between devices  1190 us (43%)
  matrix products  959 us (35%)
  other arithmetic  432 us (16%)
  local copies, waits for them, and re-layouts  83 us (3%)
  blocking collectives  40.9 us (1%)
  loops' own time  39.9 us (1%)
    dot_general x8, matrix products, block_scores(): jnp.einsum('qhd,khd->hqk', q_part, keys3, preferred_element_type=jnp.floa...  219 us
    convert_element_type x4, other arithmetic, attend_back(): grad_scores = (probs * (grad_probs - center)).astype(jnp.bfloat16)  212 us
    reduce_scatter x4, waiting for transfers between devices, sum_inputs(): return lax.psum_scatter(values, 'col', scatter_dimension=0, tiled=True)  195 us
    dot_general x4, matrix products, attend_back(): jnp.einsum('qhd,khd->hqk', grad_part, values3, preferred_element_type=jnp...  174 us
    reduce_scatter x4, waiting for transfers between devices, sum_branch(): return lax.psum_scatter(values, 'col', scatter_dimension=0, tiled=True)  152 us
    all_gather x4, waiting for transfers between devices, spread_rows(): return lax.all_gather(values, 'col', axis=0, tiled=True)  127 us
    all_gather x4, waiting for transfers between devices, spread_grads(): return lax.all_gather(values, 'col', axis=0, tiled=True)  114 us
    dot_general x4, matrix products, attend(): jnp.einsum('hqk,khd->qhd', probs_low, values3, preferred_element_type=jnp...  111 us
  transfers between devices with their start and end apart: 32, of which 31 were waited for; matrix products, arithmetic and copies ran while one was open for 7% of the time, Pallas kernels for 0%

commit v1 on v0

--- a/solution.py
+++ b/solution.py
@@ -9,6 +9,18 @@
 CONTS = 8
 EPSILON = 1e-05
 MASKED_SCORE = -1e30
+
+
+def gather_by_bits(x, axis, dim):
+    ways, here, turn = (lax.axis_size(axis), lax.axis_index(axis), x.shape[dim])
+    line, have = (x, 1)
+    while have < ways:
+        line = jnp.concatenate(
+            [line, lax.ppermute(line, axis, [(d, (d - have) % ways) for d in range(ways)])],
+            axis=dim,
+        )
+        have = 2 * have
+    return jnp.roll(line, here * turn, axis=dim)
 
 
 def normalize(values, gain, shift):
@@ -111,7 +123,7 @@
         projected = jnp.einsum("td,dsf->tsf", normed_all, w_qkv, preferred_element_type=jnp.float32)
         projected = (projected + bias_three[None]).astype(jnp.bfloat16)
         key_rows, value_rows = (
-            lax.all_gather(projected[:, 1], "row", axis=0, tiled=True),
+            gather_by_bits(projected[:, 1], "row", 0),
             lax.all_gather(projected[:, 2], "row", axis=0, tiled=True),
         )
         queries3 = projected[:, 0].reshape(row_rows, head_count, HEAD)

time: 2770 us -> 2790 us (level)
    ppermute x0 -> x4, waiting for transfers between devices: none -> 156 us  [gather_by_bits(): lax.ppermute(line, axis, [(d, (d - have) % ways) for d in range(ways)])]
    all_gather x2, waiting for transfers between devices: 72.1 us -> 0.01 us  [micro_step(): lax.all_gather(projected[:, 2], 'row', axis=0, tiled=True)]
    all_gather x2 -> x0, waiting for transfers between devices: 67 us -> none  [micro_step(): lax.all_gather(projected[:, 1], 'row', axis=0, tiled=True)]
  transfers between devices with their start and end apart: 32 -> 34, of which waited for: 31 -> 31; matrix products, arithmetic and copies ran while one was open for 7% -> 8% of each run, Pallas kernels for 0% -> 0%
where the time goes in v1:
time: 2790 us
  waiting for transfers between devices  1200 us (43%)
  matrix products  960 us (34%)
  other arithmetic  435 us (16%)
  local copies, waits for them, and re-layouts  103 us (4%)
  blocking collectives  40.9 us (1%)
  loops' own time  28.9 us (1%)
    dot_general x8, matrix products, block_scores(): jnp.einsum('qhd,khd->hqk', q_part, keys3, preferred_element_type=jnp.floa...  219 us
    convert_element_type x4, other arithmetic, attend_back(): grad_scores = (probs * (grad_probs - center)).astype(jnp.bfloat16)  212 us
    reduce_scatter x4, waiting for transfers between devices, sum_inputs(): return lax.psum_scatter(values, 'col', scatter_dimension=0, tiled=True)  195 us
    dot_general x4, matrix products, attend_back(): jnp.einsum('qhd,khd->hqk', grad_part, values3, preferred_element_type=jnp...  174 us
    ppermute x4, waiting for transfers between devices, gather_by_bits(): lax.ppermute(line, axis, [(d, (d - have) % ways) for d in range(ways)])  156 us
    reduce_scatter x4, waiting for transfers between devices, sum_branch(): return lax.psum_scatter(values, 'col', scatter_dimension=0, tiled=True)  151 us
    all_gather x4, waiting for transfers between devices, spread_rows(): return lax.all_gather(values, 'col', axis=0, tiled=True)  127 us
    all_gather x4, waiting for transfers between devices, spread_grads(): return lax.all_gather(values, 'col', axis=0, tiled=True)  114 us
  transfers between devices with their start and end apart: 34, of which 31 were waited for; matrix products, arithmetic and copies ran while one was open for 8% of the time, Pallas kernels for 0%

profile of v1, /device:TPU:0, one launch (start us, length us, event | category | flops | bytes accessed | tf_op | source)
XLA Modules:
  0.0 2788.6 jit_solution(6670517563155471712)
XLA Ops:
  29.1 30.1 %all-gather.18.cloned.1.call-done = bf16[1024,3,512]{2,0,1:T(8,128)(2,1)} async-done(((bf16[256,3,512]{2,0,1:T(8,128)(2,1)}), bf16[1024,3,512]{2,0,1:T(8,128)(2,1)}) %all-gather.18.cloned.1.call-update) | async-done | bytes 3145744 | tf_op jit(solution)/shard_map/all_gather | solution.py:101
  59.2 36.1 %all-gather.24.cloned.1.call-done = bf16[1024,2048]{1,0:T(8,128)(2,1)} async-done(((bf16[256,2048]{1,0:T(8,128)(2,1)}), bf16[1024,2048]{1,0:T(8,128)(2,1)}) %all-gather.24.cloned.1.call-update) | async-done | bytes 4194320 | tf_op jit(solution)/shard_map/all_gather | solution.py:103
  95.3 36.4 %all-gather.20.cloned.1.call-done = bf16[2048,1024]{1,0:T(8,128)(2,1)} async-done(((bf16[2048,256]{1,0:T(8,128)(2,1)}), bf16[2048,1024]{1,0:T(8,128)(2,1)}) %all-gather.20.cloned.1.call-update) | async-done | bytes 4194320 | tf_op jit(solution)/shard_map/all_gather | solution.py:104
  131.7 2365.6 %while.107 = (s32[]{:T(128)}, f32[1024,3,512]{2,0,1:T(8,128)}, f32[512,1024]{1,0:T(8,128)}, f32[1024,2048]{1,0:T(8,128)}, f32[2048,1024]{1,0:T(8,128)}, /*index=...) while((s32[]{:T(128)}, f32[1024,3,512]{2,0,1:T(8,128)}, ...), condition=%wide.region_32.33_spmd.clone.clone, body=%wide.region_0.32_spmd.clone.clone.sunk | while | flops 54254862336 | bytes 1509082112 | solution.py:272
  138.8 33.2 %all-gather.26.cloned.1.call-done = bf16[1024,1024]{1,0:T(8,128)(2,1)} async-done(((bf16[512,1024]{1,0:T(8,128)(2,1)}), bf16[1024,1024]{1,0:T(8,128)(2,1)}) %all-gather.26.cloned.1.call-update) | async-done | bytes 2097168 | tf_op jit(solution)/shard_map/while/body/eval_jaxpr/all_gather | solution.py:89
  206.1 56.3 %collective-permute-done.1 = bf16[2048,512]{0,1:T(8,128)(2,1)} collective-permute-done((bf16[2048,512]{0,1:T(8,128)(2,1)}, bf16[2048,512]{0,1:T(8,128)(2,1)}, u32[]{:S(2)}, u32[]{:S(2)}) %collective-permute-start.1) | collective-permute-done | bytes 2097184 | tf_op jit(solution)/shard_map/while/body/eval_jaxpr/ppermute | solution.py:19
  270.6 166.4 %while.108 = (s32[]{:T(128)}, bf16[2,512,8,64]{1,3,2,0:T(8,128)(2,1)}, f32[2,8,512]{2,1,0:T(8,128)S(1)}, s32[4096]{0:T(1024)S(1)}, s32[2]{0:T(128)S(1)}, /*index...) while((s32[]{:T(128)}, ...), condition=%wide.region_7.7_spmd.clone, body=%wide.region_3.6_spmd.clone.sunk | while | flops 4511079424 | bytes 219897072 | solution.py:144
  325.8 27.9 fusion.204
  360.8 26.2 fusion.202
  408.7 27.9 %fusion.204 = bf16[2,512,8,64]{1,3,2,0:T(8,128)(2,1)} fusion(bf16[2,512,8,64]{1,3,2,0:T(8,128)(2,1)} %get-tuple-element.1856, s32[]{:T(128)S(6)} %copy.81, bf16[4096,8,64]{0,2,1:T(8,128)(2,1)} %get-tuple-element.1877, f32[8,512,4096]{2,1,0:T(8,128)} %get-tuple-element.1821, f32[8,512]{1,0:T(8,128)S(1)} %fusion.203, ...), kind=kOutput, calls=%fused_computation.10.clone.1 | convolution fusion | flops 2231369728 | bytes 74481664 | tf_op jit(solution)/shard_map/while/body/eval_jaxpr/while/body/eval_jaxpr/hqk,khd->qhd/dot_general | solution.py:139
  444.1 53.8 %reduce-scatter.19.cloned.1.call-done = f32[512,1024]{1,0:T(8,128)} async-done(((f32[1024,1024]{1,0:T(8,128)}), f32[512,1024]{1,0:T(8,128)}) %reduce-scatter.19.cloned.1.call-update) | async-done | bytes 2097168 | tf_op jit(solution)/shard_map/while/body/eval_jaxpr/reduce_scatter | solution.py:95
  505.1 30.1 %all-gather.30.cloned.1.call-done = bf16[1024,1024]{1,0:T(8,128)(2,1)} async-done(((bf16[512,1024]{1,0:T(8,128)(2,1)}), bf16[1024,1024]{1,0:T(8,128)(2,1)}) %all-gather.30.cloned.1.call-update) | async-done | bytes 2097168 | tf_op jit(solution)/shard_map/while/body/eval_jaxpr/all_gather | solution.py:89
  592.0 54.5 %reduce-scatter.21.cloned.1.call-done = f32[512,1024]{1,0:T(8,128)} async-done(((f32[1024,1024]{1,0:T(8,128)}), f32[512,1024]{1,0:T(8,128)}) %reduce-scatter.21.cloned.1.call-update) | async-done | bytes 2097168 | tf_op jit(solution)/shard_map/while/body/eval_jaxpr/reduce_scatter | solution.py:98
  653.8 33.2 %all-gather.34.cloned.1.call-done = bf16[1024,1024]{1,0:T(8,128)(2,1)} async-done(((bf16[512,1024]{1,0:T(8,128)(2,1)}), bf16[1024,1024]{1,0:T(8,128)(2,1)}) %all-gather.34.cloned.1.call-update) | async-done | bytes 2097168 | tf_op jit(solution)/shard_map/while/body/eval_jaxpr/all_gather | solution.py:92
  692.0 396.0 %while.109 = (s32[]{:T(128)}, f32[4096,8,64]{0,2,1:T(8,128)}, f32[4096,8,64]{0,2,1:T(8,128)}, bf16[2,512,8,64]{1,3,2,0:T(8,128)(2,1)}, s32[2]{0:T(128)S(1)}, /*i...) while((s32[]{:T(128)}, f32[4096,8,64]{0,2,1:T(8,128)}, ...), condition=%wide.region_17.17_spmd.clone.clone, body=%wide.region_14.16_spmd.clone.clone.sunk | while | flops 10913946624 | bytes 590913280 | solution.py:208
  699.4 28.7 %subtract_exponential_fusion.3 = f32[8,512,4096]{2,1,0:T(8,128)} fusion(bf16[4096,8,64]{0,2,1:T(8,128)(2,1)} %get-tuple-element.1922, f32[8,512]{1,0:T(8,128)S(1)} %dynamic-slice_bitcast_fusion.2, pred[512,4096]{1,0:T(8,128)(4,1)S(1)} %and_or_fusion.5, bf16[1024,8,64]{0,2,1:T(8,128)(2,1)S(1)} %get-tuple-element.1918, s32[]{:T(128)S(6)} %select_n.291), kind=kOutput, calls=%fused_computation.40.clone.1 | convolution fusion | flops 2197815296 | bytes 73940992 | tf_op jit(solution)/shard_map/while/body/eval_jaxpr/while/body/eval_jaxpr/qhd,khd->hqk/dot_general | solution.py:112
  754.1 43.6 %multiply_reduce_fusion.9 = (f32[8,512]{1,0:T(8,128)S(1)}, f32[8,512,4096]{2,1,0:T(8,128)}) fusion(f32[8,512,4096]{2,1,0:T(8,128)} %subtract_exponential_fusion.3, bf16[4096,8,64]{0,2,1:T(8,128)(2,1)S(1)} %copy-done, bf16[1024,8,64]{0,2,1:T(8,128)(2,1)} %get-tuple-element.1924, s32[]{:T(128)S(6)} %select_n.291), kind=kOutput, calls=%fused_computation.39.clone.2 | convolution fusion | flops 2181033984 | bytes 138952704 | tf_op jit(solution)/shard_map/while/body/eval_jaxpr/while/body/eval_jaxpr/qhd,khd->hqk/dot_general | solution.py:189
  797.7 53.0 %multiply_convert_fusion.9 = bf16[8,512,4096]{2,1,0:T(8,128)(2,1)} fusion(f32[8,512,4096]{2,1,0:T(8,128)} %subtract_exponential_fusion.3, f32[8,512,4096]{2,1,0:T(8,128)} %get-tuple-element.1840, f32[8,512]{1,0:T(8,128)S(1)} %get-tuple-element.1841), kind=kLoop, calls=%fused_computation.38.clone.1 | loop fusion | flops 50331648 | bytes 167788544 | tf_op jit(solution)/shard_map/while/body/eval_jaxpr/while/body/eval_jaxpr/convert_element_type | solution.py:193
  894.8 28.7 %subtract_exponential_fusion.3 = f32[8,512,4096]{2,1,0:T(8,128)} fusion(bf16[4096,8,64]{0,2,1:T(8,128)(2,1)} %get-tuple-element.1922, f32[8,512]{1,0:T(8,128)S(1)} %dynamic-slice_bitcast_fusion.2, pred[512,4096]{1,0:T(8,128)(4,1)S(1)} %and_or_fusion.5, bf16[1024,8,64]{0,2,1:T(8,128)(2,1)S(1)} %get-tuple-element.1918, s32[]{:T(128)S(6)} %select_n.291), kind=kOutput, calls=%fused_computation.40.clone.1 | convolution fusion | flops 2197815296 | bytes 73940992 | tf_op jit(solution)/shard_map/while/body/eval_jaxpr/while/body/eval_jaxpr/qhd,khd->hqk/dot_general | solution.py:112
  923.5 28.3 %bitcast_add_fusion.5 = f32[4096,8,64]{0,2,1:T(8,128)} fusion(f32[4096,8,64]{0,2,1:T(8,128)} %get-tuple-element.1899, f32[8,512,4096]{2,1,0:T(8,128)} %subtract_exponential_fusion.3, pred[]{:T(512)S(6)} %compare.81, bf16[1024,8,64]{0,2,1:T(8,128)(2,1)} %get-tuple-element.1924, s32[]{:T(128)S(6)} %select_n.291), kind=kOutput, calls=%fused_computation.43.clone.1 | convolution fusion | flops 2168455168 | bytes 84410376 | tf_op jit(solution)/shard_map/while/body/eval_jaxpr/while/body/eval_jaxpr/hqk,qhd->khd/dot_general | solution.py:186
  951.8 43.6 %multiply_reduce_fusion.9 = (f32[8,512]{1,0:T(8,128)S(1)}, f32[8,512,4096]{2,1,0:T(8,128)}) fusion(f32[8,512,4096]{2,1,0:T(8,128)} %subtract_exponential_fusion.3, bf16[4096,8,64]{0,2,1:T(8,128)(2,1)S(1)} %copy-done, bf16[1024,8,64]{0,2,1:T(8,128)(2,1)} %get-tuple-element.1924, s32[]{:T(128)S(6)} %select_n.291), kind=kOutput, calls=%fused_computation.39.clone.2 | convolution fusion | flops 2181033984 | bytes 138952704 | tf_op jit(solution)/shard_map/while/body/eval_jaxpr/while/body/eval_jaxpr/qhd,khd->hqk/dot_general | solution.py:189
  995.4 53.0 %multiply_convert_fusion.9 = bf16[8,512,4096]{2,1,0:T(8,128)(2,1)} fusion(f32[8,512,4096]{2,1,0:T(8,128)} %subtract_exponential_fusion.3, f32[8,512,4096]{2,1,0:T(8,128)} %get-tuple-element.1840, f32[8,512]{1,0:T(8,128)S(1)} %get-tuple-element.1841), kind=kLoop, calls=%fused_computation.38.clone.1 | loop fusion | flops 50331648 | bytes 167788544 | tf_op jit(solution)/shard_map/while/body/eval_jaxpr/while/body/eval_jaxpr/convert_element_type | solution.py:193
  1145.3 47.1 %reduce-scatter.23.cloned.1.call-done = bf16[1024,512]{1,0:T(8,128)(2,1)} async-done(((bf16[4096,512]{1,0:T(8,128)(2,1)}), bf16[1024,512]{1,0:T(8,128)(2,1)}) %reduce-scatter.23.cloned.1.call-update) | async-done | bytes 1048592 | tf_op jit(solution)/shard_map/while/body/eval_jaxpr/reduce_scatter | solution.py:218
  1261.4 44.2 %reduce-scatter.27.cloned.1.call-done = f32[512,1024]{1,0:T(8,128)} async-done(((f32[1024,1024]{1,0:T(8,128)}), f32[512,1024]{1,0:T(8,128)}) %reduce-scatter.27.cloned.1.call-update) | async-done | bytes 2097168 | tf_op jit(solution)/shard_map/while/body/eval_jaxpr/reduce_scatter | solution.py:98
  1320.2 33.2 %all-gather.26.cloned.1.call-done = bf16[1024,1024]{1,0:T(8,128)(2,1)} async-done(((bf16[512,1024]{1,0:T(8,128)(2,1)}), bf16[1024,1024]{1,0:T(8,128)(2,1)}) %all-gather.26.cloned.1.call-update) | async-done | bytes 2097168 | tf_op jit(solution)/shard_map/while/body/eval_jaxpr/all_gather | solution.py:89
  1387.5 56.3 %collective-permute-done.1 = bf16[2048,512]{0,1:T(8,128)(2,1)} collective-permute-done((bf16[2048,512]{0,1:T(8,128)(2,1)}, bf16[2048,512]{0,1:T(8,128)(2,1)}, u32[]{:S(2)}, u32[]{:S(2)}) %collective-permute-start.1) | collective-permute-done | bytes 2097184 | tf_op jit(solution)/shard_map/while/body/eval_jaxpr/ppermute | solution.py:19
  1452.0 166.5 %while.108 = (s32[]{:T(128)}, bf16[2,512,8,64]{1,3,2,0:T(8,128)(2,1)}, f32[2,8,512]{2,1,0:T(8,128)S(1)}, s32[4096]{0:T(1024)S(1)}, s32[2]{0:T(128)S(1)}, /*index...) while((s32[]{:T(128)}, ...), condition=%wide.region_7.7_spmd.clone, body=%wide.region_3.6_spmd.clone.sunk | while | flops 4511079424 | bytes 219897072 | solution.py:144
  1507.4 27.9 fusion.204
  1542.5 26.2 fusion.202
  1590.3 27.9 %fusion.204 = bf16[2,512,8,64]{1,3,2,0:T(8,128)(2,1)} fusion(bf16[2,512,8,64]{1,3,2,0:T(8,128)(2,1)} %get-tuple-element.1856, s32[]{:T(128)S(6)} %copy.81, bf16[4096,8,64]{0,2,1:T(8,128)(2,1)} %get-tuple-element.1877, f32[8,512,4096]{2,1,0:T(8,128)} %get-tuple-element.1821, f32[8,512]{1,0:T(8,128)S(1)} %fusion.203, ...), kind=kOutput, calls=%fused_computation.10.clone.1 | convolution fusion | flops 2231369728 | bytes 74481664 | tf_op jit(solution)/shard_map/while/body/eval_jaxpr/while/body/eval_jaxpr/hqk,khd->qhd/dot_general | solution.py:139
  1625.6 53.8 %reduce-scatter.19.cloned.1.call-done = f32[512,1024]{1,0:T(8,128)} async-done(((f32[1024,1024]{1,0:T(8,128)}), f32[512,1024]{1,0:T(8,128)}) %reduce-scatter.19.cloned.1.call-update) | async-done | bytes 2097168 | tf_op jit(solution)/shard_map/while/body/eval_jaxpr/reduce_scatter | solution.py:95
  1686.5 30.1 %all-gather.30.cloned.1.call-done = bf16[1024,1024]{1,0:T(8,128)(2,1)} async-done(((bf16[512,1024]{1,0:T(8,128)(2,1)}), bf16[1024,1024]{1,0:T(8,128)(2,1)}) %all-gather.30.cloned.1.call-update) | async-done | bytes 2097168 | tf_op jit(solution)/shard_map/while/body/eval_jaxpr/all_gather | solution.py:89
  1773.3 54.5 %reduce-scatter.21.cloned.1.call-done = f32[512,1024]{1,0:T(8,128)} async-done(((f32[1024,1024]{1,0:T(8,128)}), f32[512,1024]{1,0:T(8,128)}) %reduce-scatter.21.cloned.1.call-update) | async-done | bytes 2097168 | tf_op jit(solution)/shard_map/while/body/eval_jaxpr/reduce_scatter | solution.py:98
  1835.1 33.2 %all-gather.34.cloned.1.call-done = bf16[1024,1024]{1,0:T(8,128)(2,1)} async-done(((bf16[512,1024]{1,0:T(8,128)(2,1)}), bf16[1024,1024]{1,0:T(8,128)(2,1)}) %all-gather.34.cloned.1.call-update) | async-done | bytes 2097168 | tf_op jit(solution)/shard_map/while/body/eval_jaxpr/all_gather | solution.py:92
  1873.3 396.0 %while.109 = (s32[]{:T(128)}, f32[4096,8,64]{0,2,1:T(8,128)}, f32[4096,8,64]{0,2,1:T(8,128)}, bf16[2,512,8,64]{1,3,2,0:T(8,128)(2,1)}, s32[2]{0:T(128)S(1)}, /*i...) while((s32[]{:T(128)}, f32[4096,8,64]{0,2,1:T(8,128)}, ...), condition=%wide.region_17.17_spmd.clone.clone, body=%wide.region_14.16_spmd.clone.clone.sunk | while | flops 10913946624 | bytes 590913280 | solution.py:208
  1880.9 28.7 %subtract_exponential_fusion.3 = f32[8,512,4096]{2,1,0:T(8,128)} fusion(bf16[4096,8,64]{0,2,1:T(8,128)(2,1)} %get-tuple-element.1922, f32[8,512]{1,0:T(8,128)S(1)} %dynamic-slice_bitcast_fusion.2, pred[512,4096]{1,0:T(8,128)(4,1)S(1)} %and_or_fusion.5, bf16[1024,8,64]{0,2,1:T(8,128)(2,1)S(1)} %get-tuple-element.1918, s32[]{:T(128)S(6)} %select_n.291), kind=kOutput, calls=%fused_computation.40.clone.1 | convolution fusion | flops 2197815296 | bytes 73940992 | tf_op jit(solution)/shard_map/while/body/eval_jaxpr/while/body/eval_jaxpr/qhd,khd->hqk/dot_general | solution.py:112
  1935.6 43.6 %multiply_reduce_fusion.9 = (f32[8,512]{1,0:T(8,128)S(1)}, f32[8,512,4096]{2,1,0:T(8,128)}) fusion(f32[8,512,4096]{2,1,0:T(8,128)} %subtract_exponential_fusion.3, bf16[4096,8,64]{0,2,1:T(8,128)(2,1)S(1)} %copy-done, bf16[1024,8,64]{0,2,1:T(8,128)(2,1)} %get-tuple-element.1924, s32[]{:T(128)S(6)} %select_n.291), kind=kOutput, calls=%fused_computation.39.clone.2 | convolution fusion | flops 2181033984 | bytes 138952704 | tf_op jit(solution)/shard_map/while/body/eval_jaxpr/while/body/eval_jaxpr/qhd,khd->hqk/dot_general | solution.py:189
  1979.2 53.0 %multiply_convert_fusion.9 = bf16[8,512,4096]{2,1,0:T(8,128)(2,1)} fusion(f32[8,512,4096]{2,1,0:T(8,128)} %subtract_exponential_fusion.3, f32[8,512,4096]{2,1,0:T(8,128)} %get-tuple-element.1840, f32[8,512]{1,0:T(8,128)S(1)} %get-tuple-element.1841), kind=kLoop, calls=%fused_computation.38.clone.1 | loop fusion | flops 50331648 | bytes 167788544 | tf_op jit(solution)/shard_map/while/body/eval_jaxpr/while/body/eval_jaxpr/convert_element_type | solution.py:193
  2076.3 28.7 %subtract_exponential_fusion.3 = f32[8,512,4096]{2,1,0:T(8,128)} fusion(bf16[4096,8,64]{0,2,1:T(8,128)(2,1)} %get-tuple-element.1922, f32[8,512]{1,0:T(8,128)S(1)} %dynamic-slice_bitcast_fusion.2, pred[512,4096]{1,0:T(8,128)(4,1)S(1)} %and_or_fusion.5, bf16[1024,8,64]{0,2,1:T(8,128)(2,1)S(1)} %get-tuple-element.1918, s32[]{:T(128)S(6)} %select_n.291), kind=kOutput, calls=%fused_computation.40.clone.1 | convolution fusion | flops 2197815296 | bytes 73940992 | tf_op jit(solution)/shard_map/while/body/eval_jaxpr/while/body/eval_jaxpr/qhd,khd->hqk/dot_general | solution.py:112
  2105.0 28.3 %bitcast_add_fusion.5 = f32[4096,8,64]{0,2,1:T(8,128)} fusion(f32[4096,8,64]{0,2,1:T(8,128)} %get-tuple-element.1899, f32[8,512,4096]{2,1,0:T(8,128)} %subtract_exponential_fusion.3, pred[]{:T(512)S(6)} %compare.81, bf16[1024,8,64]{0,2,1:T(8,128)(2,1)} %get-tuple-element.1924, s32[]{:T(128)S(6)} %select_n.291), kind=kOutput, calls=%fused_computation.43.clone.1 | convolution fusion | flops 2168455168 | bytes 84410376 | tf_op jit(solution)/shard_map/while/body/eval_jaxpr/while/body/eval_jaxpr/hqk,qhd->khd/dot_general | solution.py:186
  2133.3 43.6 %multiply_reduce_fusion.9 = (f32[8,512]{1,0:T(8,128)S(1)}, f32[8,512,4096]{2,1,0:T(8,128)}) fusion(f32[8,512,4096]{2,1,0:T(8,128)} %subtract_exponential_fusion.3, bf16[4096,8,64]{0,2,1:T(8,128)(2,1)S(1)} %copy-done, bf16[1024,8,64]{0,2,1:T(8,128)(2,1)} %get-tuple-element.1924, s32[]{:T(128)S(6)} %select_n.291), kind=kOutput, calls=%fused_computation.39.clone.2 | convolution fusion | flops 2181033984 | bytes 138952704 | tf_op jit(solution)/shard_map/while/body/eval_jaxpr/while/body/eval_jaxpr/qhd,khd->hqk/dot_general | solution.py:189
  2176.9 53.0 %multiply_convert_fusion.9 = bf16[8,512,4096]{2,1,0:T(8,128)(2,1)} fusion(f32[8,512,4096]{2,1,0:T(8,128)} %subtract_exponential_fusion.3, f32[8,512,4096]{2,1,0:T(8,128)} %get-tuple-element.1840, f32[8,512]{1,0:T(8,128)S(1)} %get-tuple-element.1841), kind=kLoop, calls=%fused_computation.38.clone.1 | loop fusion | flops 50331648 | bytes 167788544 | tf_op jit(solution)/shard_map/while/body/eval_jaxpr/while/body/eval_jaxpr/convert_element_type | solution.py:193
  2326.6 47.0 %reduce-scatter.23.cloned.1.call-done = bf16[1024,512]{1,0:T(8,128)(2,1)} async-done(((bf16[4096,512]{1,0:T(8,128)(2,1)}), bf16[1024,512]{1,0:T(8,128)(2,1)}) %reduce-scatter.23.cloned.1.call-update) | async-done | bytes 1048592 | tf_op jit(solution)/shard_map/while/body/eval_jaxpr/reduce_scatter | solution.py:218
  2445.1 41.7 %reduce-scatter.27.cloned.1.call-done = f32[512,1024]{1,0:T(8,128)} async-done(((f32[1024,1024]{1,0:T(8,128)}), f32[512,1024]{1,0:T(8,128)}) %reduce-scatter.27.cloned.1.call-update) | async-done | bytes 2097168 | tf_op jit(solution)/shard_map/while/body/eval_jaxpr/reduce_scatter | solution.py:98
  2519.5 40.9 %all-reduce = (f32[1024]{0:T(1024)}, f32[1024]{0:T(1024)}, f32[2,1024]{1,0:T(2,128)}, f32[1024]{0:T(1024)}, f32[1024]{0:T(1024)}, /*index=5*/f32[1024]{0:T(1024)}, f32[4096]{0:T(1024)}, f32[1024]{0:T(1024)}) all-reduce(f32[1024]{0:T(1024)S(1)} %copy-done.70, ...), channel_id=1, replica_groups=mesh['dp'=4,'row'=4,'col'=2] {'dp','row','col'}, use_global_device_ids=true, to_apply=%region_33.34 | all-reduce | flops 12288 | bytes 98304 | tf_op jit(solution)/shard_map/psum | solution.py:293
  2561.9 66.5 %reduce-scatter.11.cloned.1.call-done = bf16[64,3,512]{2,0,1:T(8,128)(2,1)} async-done(((bf16[1024,3,512]{2,0,1:T(8,128)(2,1)}), bf16[64,3,512]{2,0,1:T(8,128)(2,1)}) %reduce-scatter.11.cloned.1.call-update) | async-done | bytes 196624 | tf_op jit(solution)/shard_map/reduce_scatter | solution.py:302
  2630.2 73.9 %reduce-scatter.15.cloned.1.call-done = bf16[64,2048]{1,0:T(8,128)(2,1)} async-done(((bf16[1024,2048]{1,0:T(8,128)(2,1)}), bf16[64,2048]{1,0:T(8,128)(2,1)}) %reduce-scatter.15.cloned.1.call-update) | async-done | bytes 262160 | tf_op jit(solution)/shard_map/reduce_scatter | solution.py:312
  2705.9 73.8 %reduce-scatter.17.cloned.1.call-done = bf16[2048,64]{0,1:T(8,128)(2,1)} async-done(((bf16[2048,1024]{0,1:T(8,128)(2,1)}), bf16[2048,64]{0,1:T(8,128)(2,1)}) %reduce-scatter.17.cloned.1.call-update) | async-done | bytes 262160 | tf_op jit(solution)/shard_map/reduce_scatter | solution.py:316
  (690 shorter events, 963.6 us)
Async XLA Ops:
  7.2 21.9 all-gather.22.cloned.1.call-start
  7.9 51.3 %all-gather.18.cloned.1.call-start = ((), (), s32[]{:S(2)}) async-start(), calls=%async_computation.10 | async-start | bytes 3932160 | tf_op jit(solution)/shard_map/all_gather | solution.py:101
  8.7 86.6 %all-gather.24.cloned.1.call-start = ((), (), s32[]{:S(2)}) async-start(), calls=%async_computation.13 | async-start | bytes 5242880 | tf_op jit(solution)/shard_map/all_gather | solution.py:103
  9.4 122.3 %all-gather.20.cloned.1.call-start = ((), (), s32[]{:S(2)}) async-start(), calls=%async_computation.11 | async-start | bytes 5242880 | tf_op jit(solution)/shard_map/all_gather | solution.py:104
  131.7 40.3 %all-gather.26.cloned.1.call-start = ((), (), s32[]{:S(2)}) async-start(), calls=%async_computation.18 | async-start | bytes 3145728 | tf_op jit(solution)/shard_map/while/body/eval_jaxpr/all_gather | solution.py:89
  138.8 130.6 %all-gather.28.cloned.1.call-start = ((), (), s32[]{:S(2)}) async-start(), calls=%async_computation.19 | async-start | bytes 5242880 | tf_op jit(solution)/shard_map/while/body/eval_jaxpr/all_gather | solution.py:127
  180.5 317.4 %reduce-scatter.19.cloned.1.call-start = ((), (), s32[]{:S(2)}) async-start(), calls=%async_computation.20 | async-start | bytes 6291456 | tf_op jit(solution)/shard_map/while/body/eval_jaxpr/reduce_scatter | solution.py:95
  180.6 22.6 collective-permute-start
  204.7 57.7 %collective-permute-start.1 = (bf16[2048,512]{0,1:T(8,128)(2,1)}, bf16[2048,512]{0,1:T(8,128)(2,1)}, u32[]{:S(2)}, u32[]{:S(2)}) collective-permute-start(bf16[2048,512]{0,1:T(8,128)(2,1)} %pad_maximum_fusion.10), channel_id=1, source_target_pairs={{0,4},{2,6},{4,0},{6,2},{1,5},{3,7},{5,1},{7,3},{8,12},{10,14},{12... | collective-permute-start | bytes 6291464 | tf_op jit(solution)/shard_map/while/body/eval_jaxpr/ppermute | solution.py:19
  440.6 57.3 %copy-start.73 = (f32[1024]{0:T(1024)S(1)}, f32[1024]{0:T(1024)}, u32[]{:S(2)}) copy-start(f32[1024]{0:T(1024)} %get-tuple-element.2046) | copy-start | bytes 12292 | tf_op jit(solution)/shard_map/while
  444.1 56.4 %copy-start.35 = (f32[1024]{0:T(1024)S(1)}, f32[1024]{0:T(1024)}, u32[]{:S(2)}) copy-start(f32[1024]{0:T(1024)} %get-tuple-element.2047) | copy-start | bytes 12292 | tf_op jit(solution)/shard_map/while
  444.1 56.4 %copy-start.71 = (f32[1024]{0:T(1024)S(1)}, f32[1024]{0:T(1024)}, u32[]{:S(2)}) copy-start(f32[1024]{0:T(1024)} %get-tuple-element.2048) | copy-start | bytes 12292 | tf_op jit(solution)/shard_map/while
  444.1 91.1 %all-gather.30.cloned.1.call-start = ((), (), s32[]{:S(2)}) async-start(), calls=%async_computation.21 | async-start | bytes 3145728 | tf_op jit(solution)/shard_map/while/body/eval_jaxpr/all_gather | solution.py:89
  500.1 149.5 %copy-start.1 = (f32[512,1024]{1,0:T(8,128)}, f32[512,1024]{1,0:T(8,128)S(1)}, u32[]{:S(2)}) copy-start(f32[512,1024]{1,0:T(8,128)S(1)} %get-tuple-element.1783) | copy-start | bytes 6291460 | tf_op jit(solution)/shard_map/while
  501.9 67.9 %all-gather.32.cloned.1.call-start = ((), (), s32[]{:S(2)}) async-start(), calls=%async_computation.22 | async-start | bytes 3145728 | tf_op jit(solution)/shard_map/while/body/eval_jaxpr/all_gather | solution.py:92
  505.0 141.5 %reduce-scatter.21.cloned.1.call-start = ((), (), s32[]{:S(2)}) async-start(), calls=%async_computation.23 | async-start | bytes 6291456 | tf_op jit(solution)/shard_map/while/body/eval_jaxpr/reduce_scatter | solution.py:98
  592.0 95.0 %all-gather.34.cloned.1.call-start = ((), (), s32[]{:S(2)}) async-start(), calls=%async_computation.24 | async-start | bytes 3145728 | tf_op jit(solution)/shard_map/while/body/eval_jaxpr/all_gather | solution.py:92
  653.7 491.6 %reduce-scatter.25.cloned.1.call-start = ((), (), s32[]{:S(2)}) async-start(), calls=%async_computation.26 | async-start | bytes 5242880 | tf_op jit(solution)/shard_map/while/body/eval_jaxpr/reduce_scatter | solution.py:212
  797.7 53.0 %copy-start.19 = (bf16[2,512,8,64]{1,3,2,0:T(8,128)(2,1)S(1)}, bf16[2,512,8,64]{1,3,2,0:T(8,128)(2,1)}, u32[]{:S(2)}) copy-start(bf16[2,512,8,64]{1,3,2,0:T(8,128)(2,1)} %get-tuple-element.1900) | copy-start | bytes 3145732 | tf_op jit(solution)/shard_map/while/body/eval_jaxpr/while
  995.4 53.0 %copy-start.19 = (bf16[2,512,8,64]{1,3,2,0:T(8,128)(2,1)S(1)}, bf16[2,512,8,64]{1,3,2,0:T(8,128)(2,1)}, u32[]{:S(2)}) copy-start(bf16[2,512,8,64]{1,3,2,0:T(8,128)(2,1)} %get-tuple-element.1900) | copy-start | bytes 3145732 | tf_op jit(solution)/shard_map/while/body/eval_jaxpr/while
  1100.6 91.9 %reduce-scatter.23.cloned.1.call-start = ((), (), s32[]{:S(2)}) async-start(), calls=%async_computation.25 | async-start | bytes 5242880 | tf_op jit(solution)/shard_map/while/body/eval_jaxpr/reduce_scatter | solution.py:218
  1113.4 135.6 %reduce-scatter.29.cloned.1.call-start = ((), (), s32[]{:S(2)}) async-start(), calls=%async_computation.28 | async-start | bytes 6291456 | tf_op jit(solution)/shard_map/while/body/eval_jaxpr/reduce_scatter | solution.py:95
  1126.1 179.4 %reduce-scatter.27.cloned.1.call-start = ((), (), s32[]{:S(2)}) async-start(), calls=%async_computation.27 | async-start | bytes 6291456 | tf_op jit(solution)/shard_map/while/body/eval_jaxpr/reduce_scatter | solution.py:98
  1130.3 70.1 %copy-start.17 = (bf16[1024,1,512]{2,0,1:T(8,128)(2,1)}, bf16[1024,1,512]{2,0,1:T(8,128)(2,1)S(1)}, u32[]{:S(2)}) copy-start(bf16[1024,1,512]{2,0,1:T(8,128)(2,1)S(1)} %reshape.540) | copy-start | bytes 3145732 | tf_op jit(solution)/shard_map/while
  1313.0 40.4 %all-gather.26.cloned.1.call-start = ((), (), s32[]{:S(2)}) async-start(), calls=%async_computation.18 | async-start | bytes 3145728 | tf_op jit(solution)/shard_map/while/body/eval_jaxpr/all_gather | solution.py:89
  1320.2 130.7 %all-gather.28.cloned.1.call-start = ((), (), s32[]{:S(2)}) async-start(), calls=%async_computation.19 | async-start | bytes 5242880 | tf_op jit(solution)/shard_map/while/body/eval_jaxpr/all_gather | solution.py:127
  1361.9 317.5 %reduce-scatter.19.cloned.1.call-start = ((), (), s32[]{:S(2)}) async-start(), calls=%async_computation.20 | async-start | bytes 6291456 | tf_op jit(solution)/shard_map/while/body/eval_jaxpr/reduce_scatter | solution.py:95
  1361.9 22.6 collective-permute-start
  1386.1 57.7 %collective-permute-start.1 = (bf16[2048,512]{0,1:T(8,128)(2,1)}, bf16[2048,512]{0,1:T(8,128)(2,1)}, u32[]{:S(2)}, u32[]{:S(2)}) collective-permute-start(bf16[2048,512]{0,1:T(8,128)(2,1)} %pad_maximum_fusion.10), channel_id=1, source_target_pairs={{0,4},{2,6},{4,0},{6,2},{1,5},{3,7},{5,1},{7,3},{8,12},{10,14},{12... | collective-permute-start | bytes 6291464 | tf_op jit(solution)/shard_map/while/body/eval_jaxpr/ppermute | solution.py:19
  1622.1 57.3 %copy-start.73 = (f32[1024]{0:T(1024)S(1)}, f32[1024]{0:T(1024)}, u32[]{:S(2)}) copy-start(f32[1024]{0:T(1024)} %get-tuple-element.2046) | copy-start | bytes 12292 | tf_op jit(solution)/shard_map/while
  1625.5 56.4 %copy-start.35 = (f32[1024]{0:T(1024)S(1)}, f32[1024]{0:T(1024)}, u32[]{:S(2)}) copy-start(f32[1024]{0:T(1024)} %get-tuple-element.2047) | copy-start | bytes 12292 | tf_op jit(solution)/shard_map/while
  1625.5 56.4 %copy-start.71 = (f32[1024]{0:T(1024)S(1)}, f32[1024]{0:T(1024)}, u32[]{:S(2)}) copy-start(f32[1024]{0:T(1024)} %get-tuple-element.2048) | copy-start | bytes 12292 | tf_op jit(solution)/shard_map/while
  1625.5 91.1 %all-gather.30.cloned.1.call-start = ((), (), s32[]{:S(2)}) async-start(), calls=%async_computation.21 | async-start | bytes 3145728 | tf_op jit(solution)/shard_map/while/body/eval_jaxpr/all_gather | solution.py:89
  1681.6 149.4 %copy-start.1 = (f32[512,1024]{1,0:T(8,128)}, f32[512,1024]{1,0:T(8,128)S(1)}, u32[]{:S(2)}) copy-start(f32[512,1024]{1,0:T(8,128)S(1)} %get-tuple-element.1783) | copy-start | bytes 6291460 | tf_op jit(solution)/shard_map/while
  1683.3 67.8 %all-gather.32.cloned.1.call-start = ((), (), s32[]{:S(2)}) async-start(), calls=%async_computation.22 | async-start | bytes 3145728 | tf_op jit(solution)/shard_map/while/body/eval_jaxpr/all_gather | solution.py:92
  1686.4 141.4 %reduce-scatter.21.cloned.1.call-start = ((), (), s32[]{:S(2)}) async-start(), calls=%async_computation.23 | async-start | bytes 6291456 | tf_op jit(solution)/shard_map/while/body/eval_jaxpr/reduce_scatter | solution.py:98
  1773.2 95.0 %all-gather.34.cloned.1.call-start = ((), (), s32[]{:S(2)}) async-start(), calls=%async_computation.24 | async-start | bytes 3145728 | tf_op jit(solution)/shard_map/while/body/eval_jaxpr/all_gather | solution.py:92
  1835.0 491.5 %reduce-scatter.25.cloned.1.call-start = ((), (), s32[]{:S(2)}) async-start(), calls=%async_computation.26 | async-start | bytes 5242880 | tf_op jit(solution)/shard_map/while/body/eval_jaxpr/reduce_scatter | solution.py:212
  1979.2 53.0 %copy-start.19 = (bf16[2,512,8,64]{1,3,2,0:T(8,128)(2,1)S(1)}, bf16[2,512,8,64]{1,3,2,0:T(8,128)(2,1)}, u32[]{:S(2)}) copy-start(bf16[2,512,8,64]{1,3,2,0:T(8,128)(2,1)} %get-tuple-element.1900) | copy-start | bytes 3145732 | tf_op jit(solution)/shard_map/while/body/eval_jaxpr/while
  2176.9 53.0 %copy-start.19 = (bf16[2,512,8,64]{1,3,2,0:T(8,128)(2,1)S(1)}, bf16[2,512,8,64]{1,3,2,0:T(8,128)(2,1)}, u32[]{:S(2)}) copy-start(bf16[2,512,8,64]{1,3,2,0:T(8,128)(2,1)} %get-tuple-element.1900) | copy-start | bytes 3145732 | tf_op jit(solution)/shard_map/while/body/eval_jaxpr/while
  2281.8 91.7 %reduce-scatter.23.cloned.1.call-start = ((), (), s32[]{:S(2)}) async-start(), calls=%async_computation.25 | async-start | bytes 5242880 | tf_op jit(solution)/shard_map/while/body/eval_jaxpr/reduce_scatter | solution.py:218
  2294.7 135.6 %reduce-scatter.29.cloned.1.call-start = ((), (), s32[]{:S(2)}) async-start(), calls=%async_computation.28 | async-start | bytes 6291456 | tf_op jit(solution)/shard_map/while/body/eval_jaxpr/reduce_scatter | solution.py:95
  2307.4 179.4 %reduce-scatter.27.cloned.1.call-start = ((), (), s32[]{:S(2)}) async-start(), calls=%async_computation.27 | async-start | bytes 6291456 | tf_op jit(solution)/shard_map/while/body/eval_jaxpr/reduce_scatter | solution.py:98
  2311.5 70.0 %copy-start.17 = (bf16[1024,1,512]{2,0,1:T(8,128)(2,1)}, bf16[1024,1,512]{2,0,1:T(8,128)(2,1)S(1)}, u32[]{:S(2)}) copy-start(bf16[1024,1,512]{2,0,1:T(8,128)(2,1)S(1)} %reshape.540) | copy-start | bytes 3145732 | tf_op jit(solution)/shard_map/while
  2497.3 63.1 %reduce-scatter.13.cloned.1.call-start = ((), (), s32[]{:S(2)}) async-start(), calls=%async_computation.15 | async-start | bytes 1114112 | tf_op jit(solution)/shard_map/reduce_scatter | solution.py:306
  2500.0 128.5 %reduce-scatter.11.cloned.1.call-start = ((), (), s32[]{:S(2)}) async-start(), calls=%async_computation.14 | async-start | bytes 3342336 | tf_op jit(solution)/shard_map/reduce_scatter | solution.py:302
  2504.9 199.2 %reduce-scatter.15.cloned.1.call-start = ((), (), s32[]{:S(2)}) async-start(), calls=%async_computation.16 | async-start | bytes 4456448 | tf_op jit(solution)/shard_map/reduce_scatter | solution.py:312
  2511.1 268.6 %reduce-scatter.17.cloned.1.call-start = ((), (), s32[]{:S(2)}) async-start(), calls=%async_computation.17 | async-start | bytes 4456448 | tf_op jit(solution)/shard_map/reduce_scatter | solution.py:316
  (176 other events, 3225.4 us)
Sparse Core Ops, SparseCore 0:
  9.5 19.5 all-gather.21
  30.7 28.4 all-gather.17
  60.8 34.4 all-gather.23
  96.7 34.9 all-gather.19
  138.9 33.0 all-gather.25
  180.6 47.1 all-gather.27
  444.2 53.6 reduce-scatter.18
  502.0 33.0 all-gather.29
  536.7 33.0 all-gather.31
  592.1 54.3 reduce-scatter.20
  653.8 33.0 all-gather.33
  1100.7 44.5 reduce-scatter.24
  1147.8 44.5 reduce-scatter.22
  1194.6 54.3 reduce-scatter.28
  1251.1 54.3 reduce-scatter.26
  1320.3 33.0 all-gather.25
  1362.0 47.1 all-gather.27
  1625.6 53.6 reduce-scatter.18
  1683.5 33.0 all-gather.29
  1718.0 33.0 all-gather.31
  1773.4 54.3 reduce-scatter.20
  1835.1 33.0 all-gather.33
  2282.0 44.5 reduce-scatter.24
  2328.9 44.5 reduce-scatter.22
  2375.8 54.3 reduce-scatter.28
  2432.4 54.3 reduce-scatter.26
  2501.5 57.8 reduce-scatter.12
  2563.1 65.2 reduce-scatter.10
  2632.3 71.7 reduce-scatter.14
  2707.8 71.7 reduce-scatter.16
